TPU v7x, 32 devices: a whole 2x2x4 slice. The times are simulated.
32 devices in a mesh: tm: 8 (over z, y), stream: 4 (over x, core).
Axes of the slice: x: 2, y: 2, z: 4, core: 2. Of those that a mesh axis runs over, the one named last changes fastest.
Arguments:
- signal: bfloat16 [4, 49152, 256], P('stream', 'tm'), may hold values from -6 to 6
- lengths: int32 [4], P('stream'), may hold values from 12288 to 49152, as said below
- w_conv: bfloat16 [512, 512], replicated, may hold values from -0.25 to 0.25
- w_res: bfloat16 [256, 256], replicated, may hold values from -0.375 to 0.375
- w_in: bfloat16 [256, 1024], replicated, may hold values from -0.375 to 0.375
- w_qkv: bfloat16 [1024, 3072], P(None, 'stream')
- w_out: bfloat16 [1024, 1024], P('stream'), may hold values from -0.1875 to 0.1875
- d_out: bfloat16 [4, 192, 1024], P('stream', 'tm'), may hold values from -6 to 6
Outputs:
- out: bfloat16 [4, 192, 1024], P('stream', 'tm')
- d_signal: bfloat16 [4, 49152, 256], P('stream', 'tm')
- g_conv: float32 [512, 512], P('stream')
- g_res: float32 [256, 256], P('stream')
- g_in: float32 [256, 1024], P('stream')
- g_qkv: float32 [1024, 3072], P('tm', 'stream')
- g_out: float32 [1024, 1024], P('stream', 'tm')
Inputs may be any that keep to these rules, and one draw needn't show every extreme that they name: `lengths`: some stay has all 49152 samples valid and some other stay exactly 12288.
All inputs are finite; a program needn't handle non-finite values.
Results may differ from a plain program's by a relative error of at most 0.013.
Values may be sent and summed in bfloat16 or wider, within the bound.
A program may use at most 128 MiB of HBM per device.

v0:
```python
import math

import jax
import jax.numpy as jnp
from jax import lax
from jax.sharding import PartitionSpec as P

HEADS = 16
POOL = 256
DILATION_STEP = 512


EPS = 1e-05
HIGH = lax.Precision.HIGHEST


def shifted(value, axis, by):
    length = lax.axis_size(axis)
    pairs = [(i, i + by) for i in range(length) if 0 <= i + by < length]
    return lax.ppermute(value, axis, pairs)


def neighbour_rows(block, offset):
    return shifted(block, "tm", offset)


def local(signal, lengths, w_conv, w_res, w_in, w_qkv, w_out, d_out):
    stays, sample_values, chans = signal.shape
    width = w_in.shape[1]
    head_size = width // HEADS
    heads_here = w_out.shape[0] // head_size
    toks_here = sample_values // POOL
    scale = 1.0 / math.sqrt(head_size)
    incoming_rows = neighbour_rows(signal[:, sample_values - DILATION_STEP :], 1)
    past_rows = jnp.concatenate([incoming_rows, signal[:, : sample_values - DILATION_STEP]], axis=1)
    joined = jnp.concatenate([past_rows, signal], axis=2)
    mixed = jnp.einsum("bsc,cd->bsd", joined, w_conv, preferred_element_type=jnp.float32)
    tanh_f = jnp.tanh(mixed[..., :chans])
    sig_g = jax.nn.sigmoid(mixed[..., chans:])
    hidden = (tanh_f * sig_g).astype(jnp.bfloat16)
    sample_pos = lax.axis_index("tm") * sample_values + jnp.arange(sample_values, dtype=jnp.int32)
    valid = (sample_pos[None, :] < lengths[:, None])[..., None]
    resid = jnp.where(
        valid,
        signal.astype(jnp.float32)
        + jnp.einsum("bsc,cd->bsd", hidden, w_res, preferred_element_type=jnp.float32),
        0.0,
    )
    pooled = jnp.mean(resid.reshape(stays, toks_here, POOL, chans), axis=2).astype(jnp.bfloat16)
    own_tok = jnp.einsum("btc,cd->btd", pooled, w_in, preferred_element_type=jnp.float32).astype(
        jnp.bfloat16
    )
    group_tok, group_len = (
        lax.all_gather(own_tok, "stream", axis=0, tiled=True),
        lax.all_gather(lengths, "stream", axis=0, tiled=True),
    )
    tok_values = group_tok.astype(jnp.float32)
    tok_scale = lax.rsqrt(jnp.mean(tok_values * tok_values, axis=-1, keepdims=True) + EPS)
    normed = (tok_values * tok_scale).astype(jnp.bfloat16)
    group = normed.shape[0]
    proj = jnp.einsum("btd,de->bte", normed, w_qkv, preferred_element_type=jnp.float32).astype(
        jnp.bfloat16
    )
    proj = proj.reshape(group, toks_here, heads_here, 3, head_size)
    query = proj[:, :, :, 0]
    keyval = proj[:, :, :, 1:].reshape(group, toks_here, heads_here * 2 * head_size)
    all_kv = lax.all_gather(keyval, "tm", axis=1, tiled=True)
    total = all_kv.shape[1]
    all_kv = all_kv.reshape(group, total, heads_here, 2, head_size)
    keys = all_kv[:, :, :, 0]
    values = all_kv[:, :, :, 1]
    query_pos = lax.axis_index("tm") * toks_here + jnp.arange(toks_here, dtype=jnp.int32)
    key_pos = jnp.arange(total, dtype=jnp.int32)
    allowed = (key_pos[None, None, :] <= query_pos[None, :, None]) & (
        (key_pos * POOL)[None, None, :] < group_len[:, None, None]
    )
    scores = jnp.einsum("bqhe,bkhe->bhqk", query, keys, preferred_element_type=jnp.float32) * scale
    scores = jnp.where(allowed[:, None], scores, -1e30)
    top = jnp.max(scores, axis=-1, keepdims=True)
    weights = jnp.exp(scores - top)
    prob = weights / jnp.sum(weights, axis=-1, keepdims=True)
    prob16 = prob.astype(jnp.bfloat16)
    context = jnp.einsum(
        "bhqk,bkhe->bqhe", prob16, values, preferred_element_type=jnp.float32
    ).astype(jnp.bfloat16)
    context = context.reshape(group, toks_here, heads_here * head_size)
    head_part = jnp.einsum("bte,ed->btd", context, w_out, preferred_element_type=jnp.float32)
    summed = lax.psum_scatter(head_part, "stream", scatter_dimension=0, tiled=True)
    out = (own_tok.astype(jnp.float32) + summed).astype(jnp.bfloat16)
    group_grad = lax.all_gather(d_out, "stream", axis=0, tiled=True)
    g_out_part = jnp.einsum("bte,btd->ed", context, group_grad, preferred_element_type=jnp.float32)
    d_context = jnp.einsum(
        "btd,ed->bte", group_grad, w_out, preferred_element_type=jnp.float32
    ).astype(jnp.bfloat16)
    d_context = d_context.reshape(group, toks_here, heads_here, head_size)
    d_prob = jnp.einsum("bqhe,bkhe->bhqk", d_context, values, preferred_element_type=jnp.float32)
    d_score = prob * (d_prob - jnp.sum(d_prob * prob, axis=-1, keepdims=True))
    d_query = scale * jnp.einsum(
        "bhqk,bkhe->bqhe", d_score, keys.astype(jnp.float32), precision=HIGH
    )
    d_keys = scale * jnp.einsum(
        "bhqk,bqhe->bkhe", d_score, query.astype(jnp.float32), precision=HIGH
    )
    d_values = jnp.einsum("bhqk,bqhe->bkhe", prob16, d_context, preferred_element_type=jnp.float32)
    d_kv = jnp.stack([d_keys, d_values], axis=3).reshape(group, total, heads_here * 2 * head_size)
    d_kv_own = lax.psum_scatter(d_kv, "tm", scatter_dimension=1, tiled=True).reshape(
        group, toks_here, heads_here, 2, head_size
    )
    d_proj = jnp.concatenate([d_query[:, :, :, None], d_kv_own], axis=3).reshape(
        group, toks_here, heads_here * 3 * head_size
    )
    g_qkv_part = jnp.einsum("btd,bte->de", normed.astype(jnp.float32), d_proj, precision=HIGH)
    d_normed = jnp.einsum("bte,de->btd", d_proj, w_qkv.astype(jnp.float32), precision=HIGH)
    inner = jnp.sum(d_normed * tok_values, axis=-1, keepdims=True)
    cube = tok_scale * tok_scale * tok_scale
    d_group = tok_scale * d_normed - tok_values * cube * inner / width
    own_grad = d_out.astype(jnp.float32)
    w_in_wide = w_in.astype(jnp.float32)
    d_tok = lax.psum_scatter(d_group, "stream", scatter_dimension=0, tiled=True) + own_grad
    g_in = jnp.einsum("btc,btd->cd", pooled.astype(jnp.float32), d_tok, precision=HIGH)
    d_pooled = jnp.einsum("btd,cd->btc", d_tok, w_in_wide, precision=HIGH)
    spread = jnp.repeat(d_pooled / POOL, POOL, axis=1)
    d_resid = jnp.where(valid, spread, 0.0).astype(jnp.bfloat16)
    g_res = jnp.einsum("bsc,bsd->cd", hidden, d_resid, preferred_element_type=jnp.float32)
    d_hidden = jnp.einsum("bsd,cd->bsc", d_resid, w_res, preferred_element_type=jnp.float32)
    d_mixed = jnp.concatenate(
        [d_hidden * (1.0 - tanh_f * tanh_f) * sig_g, d_hidden * tanh_f * sig_g * (1.0 - sig_g)],
        axis=2,
    ).astype(jnp.bfloat16)
    g_conv = jnp.einsum("bsc,bsd->cd", joined, d_mixed, preferred_element_type=jnp.float32)
    d_joined = jnp.einsum("bsd,cd->bsc", d_mixed, w_conv, preferred_element_type=jnp.float32)
    past_gradient = d_joined[..., :chans].astype(jnp.bfloat16)
    arriving_rows = neighbour_rows(past_gradient[:, :DILATION_STEP], -1)
    later_gradient = jnp.concatenate([past_gradient[:, DILATION_STEP:], arriving_rows], axis=1)
    d_signal = (
        d_resid.astype(jnp.float32) + d_joined[..., chans:] + later_gradient.astype(jnp.float32)
    ).astype(jnp.bfloat16)
    head_qkv, head_out = (
        lax.psum_scatter(g_qkv_part, "tm", scatter_dimension=0, tiled=True),
        lax.psum_scatter(g_out_part, "tm", scatter_dimension=1, tiled=True),
    )
    sum_conv, sum_res, sum_in = lax.psum((g_conv, g_res, g_in), ("tm", "stream"))
    parts = lax.axis_size("stream")
    index = lax.axis_index("stream")
    conv_rows = sum_conv.shape[0] // parts
    res_rows = sum_res.shape[0] // parts
    in_rows = sum_in.shape[0] // parts
    sum_conv = lax.dynamic_slice_in_dim(sum_conv, index * conv_rows, conv_rows, 0)
    sum_res = lax.dynamic_slice_in_dim(sum_res, index * res_rows, res_rows, 0)
    sum_in = lax.dynamic_slice_in_dim(sum_in, index * in_rows, in_rows, 0)
    return (out, d_signal, sum_conv, sum_res, sum_in, head_qkv, head_out)


def solution(mesh):
    in_specs = (
        P("stream", "tm", None),
        P("stream"),
        P(),
        P(),
        P(),
        P(None, "stream"),
        P("stream", None),
        P("stream", "tm", None),
    )
    out_specs = (
        P("stream", "tm", None),
        P("stream", "tm", None),
        P("stream", None),
        P("stream", None),
        P("stream", None),
        P("tm", "stream"),
        P("stream", "tm"),
    )
    return jax.shard_map(local, mesh=mesh, in_specs=in_specs, out_specs=out_specs, check_vma=False)
```

profile of v0, /device:TPU:0, one launch (start us, length us, event | category | flops | bytes accessed | tf_op | source)
XLA Modules:
  0.0 544.1 jit_solution(6773521519445546995)
XLA Ops:
  8.4 4.9 collective-permute-start
  16.0 4.9 all-reduce
  21.0 5.8 %all_gather.15 = bf16[4,24,1024]{2,1,0:T(8,128)(2,1)S(1)} all-gather(bf16[1,24,1024]{2,1,0:T(8,128)(2,1)} %param.15), channel_id=1, replica_groups=mesh['tm'=8,'stream'=4] {'stream'}, dimensions={0}, use_global_device_ids=true | all-gather | bytes 245760 | tf_op jit(solution)/shard_map/all_gather | solution.py:90
  28.8 3.6 slice.38
  32.5 6.5 %convolution_bitcast_fusion.1 = f32[1,6144,512]{1,2,0:T(8,128)S(1)} fusion(bf16[512,512]{1,0:T(8,128)(2,1)S(1)} %copy-done.17, bf16[1,6144,256]{2,1,0:T(8,128)(2,1)} %param.8, bf16[1,5632,256]{2,1,0:T(8,128)(2,1)} %slice.38, bf16[1,512,256]{2,1,0:T(8,128)(2,1)S(1)} %collective-permute-done), kind=kOutput, calls=%fused_computation.3 | convolution fusion | flops 3240099840 | bytes 19398656 | tf_op jit(solution)/shard_map/bsc,cd->bsd/dot_general | solution.py:37
  39.1 2.5 fusion.12
  41.6 2.8 copy-done.7
  44.4 5.3 fusion.3
  49.7 3.3 reduce_sum.45
  53.2 5.6 %all-gather = bf16[96,1024]{1,0:T(8,128)(2,1)S(1)} all-gather(bf16[24,1024]{1,0:T(8,128)(2,1)S(1)} %convolution_convert_fusion.2), channel_id=2, replica_groups=mesh['tm'=8,'stream'=4] {'stream'}, dimensions={0}, use_global_device_ids=true | all-gather | bytes 245760 | tf_op jit(solution)/shard_map/all_gather | solution.py:54
  60.9 32.5 %all_gather.13 = bf16[4,192,512]{2,0,1:T(4,128)(2,1)S(1)} all-gather(bf16[4,24,512]{2,0,1:T(4,128)(2,1)S(1)} %copy.29), channel_id=1, replica_groups=mesh['tm'=8,'stream'=4] {'tm'}, dimensions={1}, use_global_device_ids=true | all-gather | bytes 884736 | tf_op jit(solution)/shard_map/all_gather | solution.py:67
  96.1 2.8 fusion.59
  98.9 1.9 convolution_bitcast_fusion.6
  105.8 2.8 copy.38
  110.2 1.7 fusion.34
  112.8 83.7 %all-reduce.6.cloned.1.call-done = f32[4,192,512]{2,0,1:T(4,128)} async-done(((f32[4,192,512]{2,0,1:T(4,128)}), f32[4,192,512]{2,0,1:T(4,128)}) %all-reduce.6.cloned.1.call-update) | async-done | bytes 1572880
  201.2 2.6 fusion.20
  205.6 1.8 fusion.35
  208.6 17.2 %reduce-scatter.7.cloned.1.call-done = f32[1,24,1024]{2,1,0:T(8,128)} async-done(((f32[4,24,1024]{2,1,0:T(8,128)}), f32[1,24,1024]{2,1,0:T(8,128)}) %reduce-scatter.7.cloned.1.call-update) | async-done | bytes 98320 | tf_op jit(solution)/shard_map/reduce_scatter | solution.py:119
  230.1 5.9 %fusion.16 = f32[256,256]{1,0:T(8,128)} fusion(bf16[6144,256]{0,1:T(8,128)(2,1)} %copy-done.5, bf16[1,6144,1,1,1,1,256]{6,1,5,4,3,2,0:T(8,128)(2,1)S(1)} %bitcast.125, pred[6144]{0:T(1024)(128)(4,1)S(1)} %add_compare_fusion), kind=kOutput, calls=%fused_computation.31 | convolution fusion | flops 806879232 | bytes 6559744 | tf_op jit(solution)/shard_map/bsc,bsd->cd/dot_general | solution.py:124
  236.1 6.8 %fusion.13 = (bf16[6144,256]{0,1:T(8,128)(2,1)S(1)}, bf16[6144,256]{0,1:T(8,128)(2,1)S(1)}) fusion(f32[1,6144,512]{1,2,0:T(8,128)} %copy-done.7, bf16[6144,256]{1,0:T(8,128)(2,1)S(1)} %fusion.9, bf16[256,256]{1,0:T(8,128)(2,1)S(1)} %copy-done.24), kind=kOutput, calls=%fused_computation.28 | convolution fusion | flops 825753600 | bytes 22151168 | tf_op jit(solution)/shard_map/bsd,cd->bsc/dot_general | solution.py:125
  242.9 2.1 fusion.46
  245.9 4.5 fusion.11
  252.2 3.2 convolution_bitcast_fusion.4
  255.4 10.9 %fusion.60 = (bf16[1,6144,512]{2,1,0:T(8,128)(2,1)S(1)}, f32[1,6144,512]{2,1,0:T(8,128)}) fusion(bf16[512,512]{1,0:T(8,128)(2,1)S(1)} %copy-done.18, bf16[6144,256]{0,1:T(8,128)(2,1)} %copy-done.9, bf16[6144,256]{0,1:T(8,128)(2,1)} %copy-done.8), kind=kOutput, calls=%fused_computation.107 | convolution fusion | flops 3236954112 | bytes 25690112 | tf_op jit(solution)/shard_map/bsd,cd->bsc/dot_general | solution.py:131
  266.3 2.6 copy-done.2
  271.8 2.0 slice.55
  273.8 6.1 %collective-permute-done.1 = bf16[1,512,256]{2,1,0:T(8,128)(2,1)S(1)} collective-permute-done((bf16[1,512,256]{2,1,0:T(8,128)(2,1)S(1)}, bf16[1,512,256]{2,1,0:T(8,128)(2,1)S(1)}, u32[]{:S(2)}, u32[]{:S(2)}) %collective-permute-start.1) | collective-permute-done | bytes 262176 | tf_op jit(solution)/shard_map/ppermute | solution.py:20
  279.9 9.5 %fusion.5 = bf16[1,6144,256]{2,1,0:T(8,128)(2,1)} fusion(f32[1,6144,512]{2,1,0:T(8,128)} %get-tuple-element.19, bf16[1,512,256]{2,1,0:T(8,128)(2,1)S(1)} %collective-permute-done.1, bf16[1,5632,256]{2,1,0:T(8,128)(2,1)S(1)} %slice.55, pred[6144]{0:T(1024)(128)(4,1)S(1)} %add_compare_fusion, bf16[1,6144,256]{2,1,0:T(8,128)(2,1)} %bitcast.126), kind=kLoop, calls=%fused_computation.10 | loop fusion | flops 14155776 | bytes 15734784 | tf_op jit(solution)/shard_map/convert_element_type | solution.py:137
  289.4 103.1 %all-reduce.8.cloned.1.call-done = (f32[512,512]{1,0:T(8,128)}, f32[256,256]{1,0:T(8,128)}, f32[256,1024]{1,0:T(8,128)}) async-done(((f32[512,512]{1,0:T(8,128)}, f32[256,256]{1,0:T(8,128)}, f32[256,1024]{1,0:T(8,128)}), (f32[512,512]{1,0:T(8,128)}, f32[256,256]{1,0:T(8,128)}, f32[256,1024]{1,0:T(8,128)})) %all-reduce.8.cloned.1.call-update) | async-done | bytes 2359312 | tf_op jit(solution)/shard_map/psum | solution.py:142
  397.3 62.8 %reduce-scatter.11.cloned.1.call-done = f32[256,128]{1,0:T(8,128)} async-done(((f32[256,1024]{1,0:T(8,128)}), f32[256,128]{1,0:T(8,128)}) %reduce-scatter.11.cloned.1.call-update) | async-done | bytes 131088 | tf_op jit(solution)/shard_map/reduce_scatter | solution.py:140
  460.1 77.2 %reduce-scatter.9.cloned.1.call-done = f32[128,768]{1,0:T(8,128)} async-done(((f32[1024,768]{1,0:T(8,128)}), f32[128,768]{1,0:T(8,128)}) %reduce-scatter.9.cloned.1.call-update) | async-done | bytes 393232 | tf_op jit(solution)/shard_map/reduce_scatter | solution.py:139
  (121 shorter events, 39.4 us)
Async XLA Ops:
  7.2 52.4 %copy-start = (bf16[1024,768]{1,0:T(8,128)(2,1)S(1)}, bf16[1024,768]{1,0:T(8,128)(2,1)}, u32[]{:S(2)}) copy-start(bf16[1024,768]{1,0:T(8,128)(2,1)} %param.13) | copy-start | bytes 4718596
  7.2 25.3 %copy-start.17 = (bf16[512,512]{1,0:T(8,128)(2,1)S(1)}, bf16[512,512]{1,0:T(8,128)(2,1)}, u32[]{:S(2)}) copy-start(bf16[512,512]{1,0:T(8,128)(2,1)} %param.10) | copy-start | bytes 1572868
  7.2 189.3 %all-reduce.6.cloned.1.call-start = ((), (), s32[]{:S(2)}) async-start(), calls=%async_computation.8 | async-start | bytes 3145728
  8.4 24.1 %collective-permute-start = (bf16[1,512,256]{2,1,0:T(8,128)(2,1)S(1)}, bf16[1,512,256]{2,1,0:T(8,128)(2,1)S(1)}, u32[]{:S(2)}, u32[]{:S(2)}) collective-permute-start(bf16[1,512,256]{2,1,0:T(8,128)(2,1)S(1)} %slice.37), channel_id=1, source_target_pairs={{0,4},{4,8},{8,12},{12,16},{16,20},{20,24},{24,28},{1,5},{5,9},{9,... | collective-permute-start | bytes 786440 | tf_op jit(solution)/shard_map/ppermute | solution.py:20
  32.5 6.5 %copy-start.28 = (bf16[1,512,256]{2,1,0:T(8,128)(2,1)}, bf16[1,512,256]{2,1,0:T(8,128)(2,1)S(1)}, u32[]{:S(2)}) copy-start(bf16[1,512,256]{2,1,0:T(8,128)(2,1)S(1)} %collective-permute-done) | copy-start | bytes 786436
  39.1 5.4 copy-start.7
  39.1 5.3 copy-start.3
  39.1 5.3 copy-start.23
  44.4 5.3 copy-start.5
  53.2 6.3 %copy-start.20 = (bf16[24,1024]{1,0:T(8,128)(2,1)}, bf16[24,1024]{1,0:T(8,128)(2,1)S(1)}, u32[]{:S(2)}) copy-start(bf16[24,1024]{1,0:T(8,128)(2,1)S(1)} %convolution_convert_fusion.2) | copy-start | bytes 147460
  59.5 43.4 %copy-start.26 = (f32[4,24]{1,0:T(4,128)}, f32[4,24]{1,0:T(4,128)S(1)}, u32[]{:S(2)}) copy-start(f32[4,24]{1,0:T(4,128)S(1)} %get-tuple-element.13) | copy-start | bytes 1156
  98.9 11.3 %copy-start.25 = (f32[4,4,24]{2,1,0:T(4,128)}, f32[4,4,24]{2,1,0:T(4,128)S(1)}, u32[]{:S(2)}) copy-start(f32[4,4,24]{2,1,0:T(4,128)S(1)} %get-tuple-element.14) | copy-start | bytes 4612
  102.9 6.0 %copy-start.30 = (u32[32]{0:T(128)S(1)}, u32[32]{0:T(128)}, u32[]{:S(2)}) copy-start(u32[32]{0:T(128)} %constant.58) | copy-start | bytes 388
  108.7 117.1 %reduce-scatter.7.cloned.1.call-start = ((), (), s32[]{:S(2)}) async-start(), calls=%async_computation.5 | async-start | bytes 491520 | tf_op jit(solution)/shard_map/reduce_scatter | solution.py:119
  110.2 97.4 %copy-start.11 = (bf16[256,1024]{1,0:T(8,128)(2,1)S(1)}, bf16[256,1024]{1,0:T(8,128)(2,1)}, u32[]{:S(2)}) copy-start(bf16[256,1024]{1,0:T(8,128)(2,1)} %param.14) | copy-start | bytes 1572868
  111.9 113.9 %copy-start.19 = (bf16[1,24,1024]{2,1,0:T(8,128)(2,1)S(1)}, bf16[1,24,1024]{2,1,0:T(8,128)(2,1)}, u32[]{:S(2)}) copy-start(bf16[1,24,1024]{2,1,0:T(8,128)(2,1)} %param.15) | copy-start | bytes 147460
  201.2 24.5 %copy-start.13 = (bf16[256,1024]{1,0:T(8,128)(2,1)S(1)}, bf16[256,1024]{1,0:T(8,128)(2,1)}, u32[]{:S(2)}) copy-start(bf16[256,1024]{1,0:T(8,128)(2,1)} %param.12) | copy-start | bytes 1572868
  205.5 64.7 %reduce-scatter.5.cloned.1.call-start = ((), (), s32[]{:S(2)}) async-start(), calls=%async_computation.4 | async-start | bytes 491520 | tf_op jit(solution)/shard_map/reduce_scatter | solution.py:88
  208.5 184.0 %all-reduce.8.cloned.1.call-start = ((), (), s32[]{:S(2)}) async-start(), calls=%async_computation.9 | async-start | bytes 4718592 | tf_op jit(solution)/shard_map/psum | solution.py:142
  228.2 7.8 %copy-start.24 = (bf16[256,256]{1,0:T(8,128)(2,1)S(1)}, bf16[256,256]{1,0:T(8,128)(2,1)}, u32[]{:S(2)}) copy-start(bf16[256,256]{1,0:T(8,128)(2,1)} %param.11) | copy-start | bytes 393220
  236.1 6.8 %copy-start.22 = (f32[1,24,1024]{2,1,0:T(8,128)S(1)}, f32[1,24,1024]{2,1,0:T(8,128)}, u32[]{:S(2)}) copy-start(f32[1,24,1024]{2,1,0:T(8,128)} %reduce-scatter.7.cloned.1.call-done) | copy-start | bytes 294916
  236.1 9.8 %copy-start.4 = (bf16[1,6144,256]{2,1,0:T(8,128)(2,1)S(1)}, bf16[1,6144,256]{2,1,0:T(8,128)(2,1)}, u32[]{:S(2)}) copy-start(bf16[1,6144,256]{2,1,0:T(8,128)(2,1)} %param.8) | copy-start | bytes 9437188
  236.1 9.8 %copy-start.10 = (bf16[1,5632,256]{2,1,0:T(8,128)(2,1)S(1)}, bf16[1,5632,256]{2,1,0:T(8,128)(2,1)}, u32[]{:S(2)}) copy-start(bf16[1,5632,256]{2,1,0:T(8,128)(2,1)} %slice.38) | copy-start | bytes 8650756
  236.1 9.8 %copy-start.29 = (bf16[1,512,256]{2,1,0:T(8,128)(2,1)S(1)}, bf16[1,512,256]{2,1,0:T(8,128)(2,1)}, u32[]{:S(2)}) copy-start(bf16[1,512,256]{2,1,0:T(8,128)(2,1)} %copy-done.28) | copy-start | bytes 786436
  245.9 6.3 %copy-start.14 = (f32[4,24,768]{2,1,0:T(8,128)S(1)}, f32[4,24,768]{2,1,0:T(8,128)}, u32[]{:S(2)}) copy-start(f32[4,24,768]{2,1,0:T(8,128)} %reshape.321) | copy-start | bytes 884740
  245.9 6.3 %copy-start.27 = (f32[4,24]{1,0:T(4,128)S(1)}, f32[4,24]{1,0:T(4,128)}, u32[]{:S(2)}) copy-start(f32[4,24]{1,0:T(4,128)} %copy-done.26) | copy-start | bytes 1156
  250.4 5.0 copy-start.18
  250.4 209.7 %reduce-scatter.11.cloned.1.call-start = ((), (), s32[]{:S(2)}) async-start(), calls=%async_computation.7 | async-start | bytes 1179648 | tf_op jit(solution)/shard_map/reduce_scatter | solution.py:140
  251.9 285.4 %reduce-scatter.9.cloned.1.call-start = ((), (), s32[]{:S(2)}) async-start(), calls=%async_computation.6 | async-start | bytes 3538944 | tf_op jit(solution)/shard_map/reduce_scatter | solution.py:139
  255.4 14.8 %copy-start.21 = (bf16[24,1024]{1,0:T(8,128)(2,1)S(1)}, bf16[24,1024]{1,0:T(8,128)(2,1)}, u32[]{:S(2)}) copy-start(bf16[24,1024]{1,0:T(8,128)(2,1)} %copy-done.20) | copy-start | bytes 147460
  268.9 11.0 %collective-permute-start.1 = (bf16[1,512,256]{2,1,0:T(8,128)(2,1)S(1)}, bf16[1,512,256]{2,1,0:T(8,128)(2,1)S(1)}, u32[]{:S(2)}, u32[]{:S(2)}) collective-permute-start(bf16[1,512,256]{2,1,0:T(8,128)(2,1)S(1)} %slice.56), channel_id=1, source_target_pairs={{4,0},{8,4},{12,8},{16,12},{20,16},{24,20},{28,24},{5,1},{9,5},{13... | collective-permute-start | bytes 786440 | tf_op jit(solution)/shard_map/ppermute | solution.py:20
  279.9 257.4 %copy-start.1 = (bf16[1024,768]{1,0:T(8,128)(2,1)S(1)}, bf16[1024,768]{1,0:T(8,128)(2,1)}, u32[]{:S(2)}) copy-start(bf16[1024,768]{1,0:T(8,128)(2,1)} %param.13) | copy-start | bytes 4718596
  (7 other events, 17.9 us)
Sparse Core Ops, SparseCore 0:
  108.8 87.6 all-reduce.5
  205.6 20.0 reduce-scatter.6
  228.2 20.8 reduce-scatter.4
  255.4 137.0 all-reduce.7
  396.3 63.7 reduce-scatter.10
  464.1 73.0 reduce-scatter.8
where the time goes:
time: 545 us; the launch traced here: 544 us
  waiting for transfers between devices  350 us (64%)
  matrix products  62.2 us (11%)
  blocking collectives  48.8 us (9%)
  local copies, waits for them, and re-layouts  34.1 us (6%)
  other arithmetic  26.2 us (5%)
  between operations  15.9 us (3%)
  starting transfers between devices  6.85 us (1%)
    psum x1, waiting for transfers between devices, local(): lax.psum((g_conv, g_res, g_in), ('tm', 'stream'))  103 us
    unnamed x7, waiting for transfers between devices  83.8 us
    reduce_scatter x1, waiting for transfers between devices, local(): lax.psum_scatter(g_qkv_part, 'tm', scatter_dimension=0, tiled=True)  77.2 us
    reduce_scatter x1, waiting for transfers between devices, local(): lax.psum_scatter(g_out_part, 'tm', scatter_dimension=1, tiled=True)  62.8 us
    all_gather x1, blocking collectives, local(): all_kv = lax.all_gather(keyval, 'tm', axis=1, tiled=True)  32.5 us
    reduce_scatter x1, waiting for transfers between devices, local(): lax.psum_scatter(d_group, 'stream', scatter_dimension=0, tiled=True)  17.2 us
    unnamed x67, local copies, waits for them, and re-layouts  12.2 us
  transfers between devices with their start and end apart: 8, of which 6 were waited for; matrix products, arithmetic and copies ran while one was open for 13% of the time, Pallas kernels for 0%

commit v1 on v0

v1 whole, which is shorter than its diff:
```python
import functools
import math

import jax
import jax.numpy as jnp
from jax import lax
from jax.experimental import pallas as pl
from jax.experimental.pallas import tpu as pltpu
from jax.sharding import PartitionSpec as P

HEADS = 16
POOL = 256
DILATION_STEP = 512
EPS = 1e-05
BF16 = jnp.bfloat16
F32 = jnp.float32
MESH = pl.DeviceIdType.MESH
VMEM_SPEC = pl.BlockSpec(memory_space=pltpu.VMEM)


def dot(eq, a, b):
    return jnp.einsum(eq, a, b, preferred_element_type=F32)


def exchange_kernel(axis, n, kinds, *refs):
    k = len(kinds)
    ins, outs = refs[:k], refs[k : 2 * k]
    rest = list(refs[2 * k :])
    slots = [rest.pop(0) if kind == "reduce" else None for kind in kinds]
    send, recv, local_sem = rest
    me = lax.axis_index(axis)
    barrier = pltpu.get_barrier_semaphore()
    for d in range(1, n):
        pl.semaphore_signal(
            barrier, inc=1, device_id={axis: lax.rem(me + d, n)}, device_id_type=MESH
        )
    pl.semaphore_wait(barrier, n - 1)
    copies = []
    locals_ = []
    for j, kind in enumerate(kinds):
        for d in range(1, n):
            peer = lax.rem(me + d, n)
            src = ins[j] if kind.startswith("gather") else ins[j].at[peer]
            if kind == "reduce":
                dst = slots[j].at[d - 1]
            elif kind.endswith("1"):
                dst = outs[j].at[:, me]
            else:
                dst = outs[j].at[me]
            copy = pltpu.make_async_remote_copy(
                src_ref=src,
                dst_ref=dst,
                send_sem=send.at[j, d - 1],
                recv_sem=recv.at[j, d - 1],
                device_id={axis: peer},
                device_id_type=MESH,
            )
            copy.start()
            copies.append(copy)
        if kind != "reduce":
            src = ins[j] if kind.startswith("gather") else ins[j].at[me]
            dst = outs[j].at[:, me] if kind.endswith("1") else outs[j].at[me]
            copy = pltpu.make_async_copy(src, dst, local_sem.at[j])
            copy.start()
            locals_.append(copy)
    for copy in locals_:
        copy.wait()
    for copy in copies:
        copy.wait()
    for j, kind in enumerate(kinds):
        if kind == "reduce":
            total = ins[j][me].astype(F32)
            for d in range(1, n):
                total += slots[j][d - 1].astype(F32)
            outs[j][...] = total


def exchange(axis, collective, items):
    n = lax.axis_size(axis)
    kinds = tuple(kind for kind, _ in items)
    arrays = [array for _, array in items]
    shapes, slots = [], []
    for kind, array in items:
        inner = array.shape if kind.startswith("gather") else array.shape[1:]
        if kind == "reduce":
            shapes.append(jax.ShapeDtypeStruct(inner, F32))
            slots.append(pltpu.VMEM((n - 1,) + inner, array.dtype))
        elif kind.endswith("1"):
            shapes.append(jax.ShapeDtypeStruct((inner[0], n) + inner[1:], array.dtype))
        else:
            shapes.append(jax.ShapeDtypeStruct((n,) + inner, array.dtype))
    k = len(items)
    return pl.pallas_call(
        functools.partial(exchange_kernel, axis, n, kinds),
        out_shape=shapes,
        in_specs=[VMEM_SPEC] * k,
        out_specs=[VMEM_SPEC] * k,
        scratch_shapes=slots
        + [
            pltpu.SemaphoreType.DMA((k, n - 1)),
            pltpu.SemaphoreType.DMA((k, n - 1)),
            pltpu.SemaphoreType.DMA((k,)),
        ],
        compiler_params=pltpu.CompilerParams(collective_id=collective, has_side_effects=True),
        name=f"exchange_{axis}_{collective}",
    )(*arrays)


def attention_kernel(heads, size, scale, len_ref, proj_ref, dctx_ref, ctx_ref, dproj_ref):
    stay = pl.program_id(0)
    total = proj_ref.shape[1]
    length = len_ref[stay]
    row = lax.broadcasted_iota(jnp.int32, (total, total), 0)
    col = lax.broadcasted_iota(jnp.int32, (total, total), 1)
    allowed = (col <= row) & (col * POOL < length)
    nt = (((1,), (1,)), ((), ()))
    tn = (((0,), (0,)), ((), ()))
    for h in range(heads):
        base = h * 3 * size
        query = proj_ref[0, :, base : base + size]
        key = proj_ref[0, :, base + size : base + 2 * size]
        value = proj_ref[0, :, base + 2 * size : base + 3 * size]
        dctx = dctx_ref[0, :, h * size : (h + 1) * size]
        scores = lax.dot_general(query, key, nt, preferred_element_type=F32) * scale
        scores = jnp.where(allowed, scores, -1e30)
        top = jnp.max(scores, axis=-1, keepdims=True)
        weights = jnp.exp(scores - top)
        prob = weights / jnp.sum(weights, axis=-1, keepdims=True)
        prob16 = prob.astype(BF16)
        context = jnp.dot(prob16, value, preferred_element_type=F32)
        ctx_ref[0, :, h * size : (h + 1) * size] = context.astype(BF16)
        d_prob = lax.dot_general(dctx, value, nt, preferred_element_type=F32)
        d_score = prob * (d_prob - jnp.sum(d_prob * prob, axis=-1, keepdims=True))
        d16 = d_score.astype(BF16)
        d_query = scale * jnp.dot(d16, key, preferred_element_type=F32)
        d_key = scale * lax.dot_general(d16, query, tn, preferred_element_type=F32)
        d_value = lax.dot_general(prob16, dctx, tn, preferred_element_type=F32)
        dproj_ref[0, :, base : base + size] = d_query.astype(BF16)
        dproj_ref[0, :, base + size : base + 2 * size] = d_key.astype(BF16)
        dproj_ref[0, :, base + 2 * size : base + 3 * size] = d_value.astype(BF16)


def attention(proj, d_context, group_len, heads, size):
    group, total, width = proj.shape
    inner = heads * size
    wide = pl.BlockSpec((1, total, width), lambda s: (s, 0, 0))
    thin = pl.BlockSpec((1, total, inner), lambda s: (s, 0, 0))
    return pl.pallas_call(
        functools.partial(attention_kernel, heads, size, 1.0 / math.sqrt(size)),
        grid=(group,),
        out_shape=(
            jax.ShapeDtypeStruct((group, total, inner), BF16),
            jax.ShapeDtypeStruct((group, total, width), BF16),
        ),
        in_specs=[pl.BlockSpec(memory_space=pltpu.SMEM), wide, thin],
        out_specs=(thin, wide),
        name="attention",
    )(group_len, proj, d_context)


def shifted(value, axis, by):
    length = lax.axis_size(axis)
    pairs = [(i, i + by) for i in range(length) if 0 <= i + by < length]
    return lax.ppermute(value, axis, pairs)


def local(signal, lengths, w_conv, w_res, w_in, w_qkv, w_out, d_out):
    stays, samples, chans = signal.shape
    width = w_in.shape[1]
    size = width // HEADS
    heads = w_out.shape[0] // size
    toks = samples // POOL
    tms, parts = lax.axis_size("tm"), lax.axis_size("stream")
    tm = lax.axis_index("tm")
    group = stays * parts
    total = toks * tms
    incoming = shifted(signal[:, samples - DILATION_STEP :], "tm", 1)
    past = jnp.concatenate([incoming, signal[:, : samples - DILATION_STEP]], axis=1)
    joined = jnp.concatenate([past, signal], axis=2)
    mixed = dot("bsc,cd->bsd", joined, w_conv)
    tanh_f = jnp.tanh(mixed[..., :chans])
    sig_g = jax.nn.sigmoid(mixed[..., chans:])
    hidden = (tanh_f * sig_g).astype(BF16)
    pos = tm * samples + jnp.arange(samples, dtype=jnp.int32)
    valid = (pos[None, :] < lengths[:, None])[..., None]
    resid = jnp.where(valid, signal.astype(F32) + dot("bsc,cd->bsd", hidden, w_res), 0.0)
    pooled = jnp.mean(resid.reshape(stays, toks, POOL, chans), axis=2).astype(BF16)
    own_tok = dot("btc,cd->btd", pooled, w_in).astype(BF16)
    lens8 = jnp.broadcast_to(lengths.reshape(stays, 1, 1), (stays, 8, 128))
    g_pool, g_dout, g_len = exchange(
        "stream", 0, [("gather", pooled), ("gather", d_out), ("gather", lens8)]
    )
    group_pool = g_pool.reshape(group, toks, chans)
    group_grad = g_dout.reshape(group, toks, width)
    group_len = g_len.reshape(group, 8, 128)[:, 0, 0]
    d_ctx = dot("btd,ed->bte", group_grad, w_out).astype(BF16)
    columns = width // tms
    grad_cols = group_grad.reshape(group, toks, tms, columns).transpose(2, 0, 1, 3)
    all_pool, all_ctx, all_cols = exchange(
        "tm", 1, [("gather1", group_pool), ("gather1", d_ctx), ("scatter1", grad_cols)]
    )
    all_pool = all_pool.reshape(group, total, chans)
    all_ctx = all_ctx.reshape(group, total, heads * size)
    all_cols = all_cols.reshape(group, total, columns)
    tok = dot("btc,cd->btd", all_pool, w_in).astype(BF16).astype(F32)
    r = lax.rsqrt(jnp.mean(tok * tok, axis=-1, keepdims=True) + EPS)
    normed = (tok * r).astype(BF16)
    proj = dot("btd,de->bte", normed, w_qkv).astype(BF16)
    context, d_proj = attention(proj, all_ctx, group_len, heads, size)
    own_ctx = lax.dynamic_slice_in_dim(context, tm * toks, toks, 1)
    out_part = dot("bte,ed->btd", own_ctx, w_out).astype(BF16)
    g_out = dot("bte,btd->ed", context, all_cols)
    own_norm = lax.dynamic_slice_in_dim(normed, tm * columns, columns, 2)
    g_qkv = dot("btd,bte->de", own_norm, d_proj)
    d_normed = dot("bte,de->btd", d_proj, w_qkv)
    inner = jnp.sum(d_normed * tok, axis=-1, keepdims=True)
    d_group = (r * d_normed - tok * (r * r * r) * inner / width).astype(BF16)
    own_group = lax.dynamic_slice_in_dim(d_group, tm * toks, toks, 1)
    g_in_part = dot("btc,btd->cd", all_pool, d_group).astype(BF16)
    in_rows = chans // parts
    g_in_cols = dot("btc,btd->cd", all_pool, all_cols)
    stream = lax.axis_index("stream")
    g_in_cols = lax.dynamic_slice_in_dim(g_in_cols, stream * in_rows, in_rows, 0)
    s_out, s_group, s_in = exchange(
        "stream",
        2,
        [
            ("reduce", out_part.reshape(parts, stays, toks, width)),
            ("reduce", own_group.reshape(parts, stays, toks, width)),
            ("reduce", g_in_part.reshape(parts, in_rows, width)),
        ],
    )
    out = (own_tok.astype(F32) + s_out).astype(BF16)
    d_tok = (s_group + d_out.astype(F32)).astype(BF16)
    d_pooled = dot("btd,cd->btc", d_tok, w_in)
    spread = jnp.repeat(d_pooled / POOL, POOL, axis=1)
    d_resid = jnp.where(valid, spread, 0.0).astype(BF16)
    g_res = dot("bsc,bsd->cd", hidden, d_resid)
    d_hidden = dot("bsd,cd->bsc", d_resid, w_res)
    d_mixed = jnp.concatenate(
        [d_hidden * (1.0 - tanh_f * tanh_f) * sig_g, d_hidden * tanh_f * sig_g * (1.0 - sig_g)],
        axis=2,
    ).astype(BF16)
    g_conv = dot("bsc,bsd->cd", joined, d_mixed)
    d_joined = dot("bsd,cd->bsc", d_mixed, w_conv)
    past_grad = d_joined[..., :chans].astype(BF16)
    arriving = shifted(past_grad[:, :DILATION_STEP], "tm", -1)
    later = jnp.concatenate([past_grad[:, DILATION_STEP:], arriving], axis=1)
    d_signal = (d_resid.astype(F32) + d_joined[..., chans:] + later.astype(F32)).astype(BF16)
    s_conv, s_res = exchange(
        "stream",
        3,
        [
            ("reduce", g_conv.astype(BF16).reshape(parts, -1, 2 * chans)),
            ("reduce", g_res.astype(BF16).reshape(parts, -1, chans)),
        ],
    )
    t_conv, t_res = exchange(
        "tm",
        4,
        [
            ("reduce", s_conv.astype(BF16).reshape(tms, -1, 2 * chans)),
            ("reduce", s_res.astype(BF16).reshape(tms, -1, chans)),
        ],
    )
    a_conv, a_res, a_in = exchange(
        "tm",
        5,
        [
            ("gather", t_conv.astype(BF16)),
            ("gather", t_res.astype(BF16)),
            ("gather", g_in_cols.astype(BF16)),
        ],
    )
    sum_conv = a_conv.reshape(2 * chans // parts, 2 * chans).astype(F32)
    sum_res = a_res.reshape(chans // parts, chans).astype(F32)
    sum_in = s_in + a_in.transpose(1, 0, 2).reshape(in_rows, width).astype(F32)
    return (out, d_signal, sum_conv, sum_res, sum_in, g_qkv, g_out)


def solution(mesh):
    in_specs = (
        P("stream", "tm", None),
        P("stream"),
        P(),
        P(),
        P(),
        P(None, "stream"),
        P("stream", None),
        P("stream", "tm", None),
    )
    out_specs = (
        P("stream", "tm", None),
        P("stream", "tm", None),
        P("stream", None),
        P("stream", None),
        P("stream", None),
        P("tm", "stream"),
        P("stream", "tm"),
    )
    return jax.shard_map(local, mesh=mesh, in_specs=in_specs, out_specs=out_specs, check_vma=False)
```

time: 545 us -> 206 us (0.38)
  waiting for transfers between devices: 350 us -> 2.66 us
  Pallas kernels: 0 us -> 98.3 us
  blocking collectives: 48.8 us -> 0 us
  local copies, waits for them, and re-layouts: 34.1 us -> 17.6 us
  between operations: 15.9 us -> 1.67 us
  matrix products: 62.2 us -> 50.1 us
    reduce_scatter x4 -> x0, waiting for transfers between devices: 157 us -> none  [the longest x1 77.2 us: local(): lax.psum_scatter(g_qkv_part, 'tm', scatter_dimension=0, tiled=True)]
    psum x1 -> x0, waiting for transfers between devices: 103 us -> none  [local(): lax.psum((g_conv, g_res, g_in), ('tm', 'stream'))]
    pallas_call x0 -> x7, Pallas kernels: none -> 98.3 us  [the longest x6 85.8 us: exchange(): pl.pallas_call(functools.partial(exchange_kernel, axis, n, kinds), out_sh...]
    unnamed x7 -> x0, waiting for transfers between devices: 83.8 us -> none
    all_gather x3 -> x0, blocking collectives: 43.9 us -> none  [the longest x1 32.5 us: local(): all_kv = lax.all_gather(keyval, 'tm', axis=1, tiled=True)]
    dot_general x21 -> x17, matrix products: 62.2 us -> 50.1 us  [dot(): return jnp.einsum(eq, a, b, preferred_element_type=F32)]
    unnamed x67 -> x53, local copies, waits for them, and re-layouts: 12.2 us -> 5.56 us
    convert_element_type x3 -> x9, other arithmetic: 12.1 us -> 18.3 us  [the longest x1 9.05 us: local(): (d_resid.astype(F32) + d_joined[..., chans:] + later.astype(F32)).astype(...]
  transfers between devices with their start and end apart: 8 -> 2, of which waited for: 6 -> 2; matrix products, arithmetic and copies ran while one was open for 13% -> 4% of each run, Pallas kernels for 0% -> 0%
where the time goes in v1:
time: 206 us; the launch traced here: 205 us
  Pallas kernels  98.3 us (48%)
  matrix products  50.1 us (24%)
  other arithmetic  28.7 us (14%)
  local copies, waits for them, and re-layouts  17.6 us (9%)
  starting transfers between devices  6.21 us (3%)
  waiting for transfers between devices  2.66 us (1%)
    pallas_call x6, Pallas kernels, exchange(): pl.pallas_call(functools.partial(exchange_kernel, axis, n, kinds), out_sh...  85.8 us
    dot_general x17, matrix products, dot(): return jnp.einsum(eq, a, b, preferred_element_type=F32)  50.1 us
    pallas_call x1, Pallas kernels, attention(): pl.pallas_call(functools.partial(attention_kernel, heads, size, 1.0 / mat...  12.5 us
    convert_element_type x1, other arithmetic, local(): (d_resid.astype(F32) + d_joined[..., chans:] + later.astype(F32)).astype(...  9.05 us
    ppermute x2, starting transfers between devices, shifted(): return lax.ppermute(value, axis, pairs)  6.21 us
    unnamed x53, local copies, waits for them, and re-layouts  5.56 us
  transfers between devices with their start and end apart: 2, of which 2 were waited for; matrix products, arithmetic and copies ran while one was open for 4% of the time, Pallas kernels for 0%

profile of v1, /device:TPU:0, one launch (start us, length us, event | category | flops | bytes accessed | tf_op | source)
XLA Modules:
  0.0 205.3 jit_solution(1486092438006160836)
XLA Ops:
  1.8 4.9 %collective-permute-start = (bf16[1,512,256]{2,1,0:T(8,128)(2,1)S(1)}, bf16[1,512,256]{2,1,0:T(8,128)(2,1)S(1)}, u32[]{:S(2)}, u32[]{:S(2)}) collective-permute-start(bf16[1,512,256]{2,1,0:T(8,128)(2,1)S(1)} %slice.28), channel_id=1, source_target_pairs={{0,4},{4,8},{8,12},{12,16},{16,20},{20,24},{24,28},{1,5},{5,9},{9,... | collective-permute-start | bytes 786440 | tf_op jit(solution)/shard_map/ppermute | solution.py:164
  6.7 3.6 %slice.29 = bf16[1,5632,256]{2,1,0:T(8,128)(2,1)} slice(bf16[1,6144,256]{2,1,0:T(8,128)(2,1)} %param.8), slice={[0:1], [0:5632], [0:256]} | slice | bytes 5767168 | tf_op jit(solution)/shard_map/slice | solution.py:178
  12.2 6.5 %convolution_bitcast_fusion.1 = f32[1,6144,512]{1,2,0:T(8,128)S(1)} fusion(bf16[512,512]{1,0:T(8,128)(2,1)S(1)} %copy-done.16, bf16[1,6144,256]{2,1,0:T(8,128)(2,1)} %param.8, bf16[1,5632,256]{2,1,0:T(8,128)(2,1)} %slice.29, bf16[1,512,256]{2,1,0:T(8,128)(2,1)S(1)} %collective-permute-done), kind=kOutput, calls=%fused_computation.2 | convolution fusion | flops 3240099840 | bytes 19398656 | tf_op jit(solution)/shard_map/bsc,cd->bsd/dot_general | solution.py:22
  18.8 2.5 %fusion.17 = bf16[6144,256]{0,1:T(8,128)(2,1)S(1)} fusion(f32[1,6144,512]{1,2,0:T(8,128)S(1)} %convolution_bitcast_fusion.1), kind=kLoop, calls=%fused_computation.36 | loop fusion | flops 7864320 | bytes 15728640 | tf_op jit(solution)/shard_map/reshape.4
  21.3 2.8 %copy-done.8 = f32[1,6144,512]{1,2,0:T(8,128)} copy-done((f32[1,6144,512]{1,2,0:T(8,128)}, f32[1,6144,512]{1,2,0:T(8,128)S(1)}, u32[]{:S(2)}) %copy-start.8) | copy-done | bytes 12582936
  24.1 5.3 %fusion.2 = f32[1,6144,256]{2,1,0:T(8,128)} fusion(bf16[6144,256]{0,1:T(8,128)(2,1)S(1)} %fusion.17, bf16[256,256]{1,0:T(8,128)(2,1)S(1)} %copy-done.21, bf16[1,6144,256]{2,1,0:T(8,128)(2,1)S(1)} %copy-done.2, pred[6144]{0:T(1024)(128)(4,1)S(1)} %add_compare_fusion), kind=kOutput, calls=%fused_computation.6 | convolution fusion | flops 810024960 | bytes 12720128 | tf_op jit(solution)/shard_map/bsc,cd->bsd/dot_general | solution.py:22
  29.4 3.3 %reduce_sum.27 = f32[24,256]{1,0:T(8,128)S(1)} reduce(f32[24,256,256]{2,1,0:T(8,128)} %bitcast.147, f32[]{:T(128)} %constant.10.clone.1), dimensions={1}, to_apply=%region_0.1 | reduce | flops 1566720 | bytes 6316036 | tf_op jit(solution)/shard_map/reduce_sum | solution.py:187
  33.9 7.5 %exchange_stream_0.1 = (bf16[4,1,24,256]{3,2,1,0:T(8,128)(2,1)}, bf16[4,1,24,1024]{3,2,1,0:T(8,128)(2,1)}, s32[4,1,8,128]{3,2,1,0:T(8,128)}) custom-call(bf16[1,24,256]{2,1,0:T(8,128)(2,1)} %fusion.51.refs_0_, bf16[1,24,1024]{2,1,0:T(8,128)(2,1)} %refs_1_.1, s32[1,8,128]{2,1,0:T(8,128)} %broadcast_in_dim.45.refs_2_), custom_call_target="tpu_custom_call" | custom-call | tf_op jit(solution)/shard_map/exchange_stream_0/pallas_call | solution.py:93
  42.8 1.8 convolution_convert_fusion.2.refs_1_
  46.3 29.6 %exchange_tm_1.1 = (bf16[4,8,24,256]{3,2,1,0:T(8,128)(2,1)}, bf16[4,8,24,256]{3,2,1,0:T(8,128)(2,1)}, bf16[4,8,24,128]{3,2,1,0:T(8,128)(2,1)}) custom-call(bf16[4,24,256]{2,1,0:T(8,128)(2,1)} %bitcast.159, bf16[4,24,256]{2,1,0:T(8,128)(2,1)} %convolution_convert_fusion.2.refs_1_, bf16[8,4,24,128]{3,2,1,0:T(8,128)(2,1)} %bitcast.150), custom_call_target="tpu_custom_call" | custom-call | tf_op jit(solution)/shard_map/exchange_tm_1/pallas_call | solution.py:93
  77.2 1.7 fusion.11
  79.3 2.4 %fusion.30.proj_ref = bf16[4,192,768]{2,1,0:T(8,128)(2,1)} fusion(bf16[4,192,1024]{2,1,0:T(8,128)(2,1)S(1)} %fusion.12, bf16[1024,768]{1,0:T(8,128)(2,1)S(1)} %copy-done), kind=kOutput, calls=%fused_computation.49 | convolution fusion | flops 1208549376 | bytes 4325376 | tf_op jit(solution)/shard_map/btd,de->bte/dot_general | solution.py:22
  81.7 12.5 %attention.1 = (bf16[4,192,256]{2,1,0:T(8,128)(2,1)}, bf16[4,192,768]{2,1,0:T(8,128)(2,1)}) custom-call(s32[4]{0:T(128)} %slice_reduce_fusion.len_ref, bf16[4,192,768]{2,1,0:T(8,128)(2,1)} %fusion.30.proj_ref, bf16[4,192,256]{2,1,0:T(8,128)(2,1)} %bitcast.156), custom_call_target="tpu_custom_call" | custom-call | tf_op jit(solution)/shard_map/attention/pallas_call | solution.py:148
  94.2 2.8 %fusion.26 = f32[4,192,1024]{2,1,0:T(8,128)S(1)} fusion(bf16[4,192,768]{2,1,0:T(8,128)(2,1)} %get-tuple-element.31, bf16[1024,768]{1,0:T(8,128)(2,1)S(1)} %copy-done), kind=kOutput, calls=%fused_computation.45 | convolution fusion | flops 1207959552 | bytes 5898240 | tf_op jit(solution)/shard_map/bte,de->btd/dot_general | solution.py:22
  97.0 2.0 convolution_bitcast_fusion.5
  99.1 1.5 fusion.16
  100.6 1.4 fusion.33
  103.6 14.1 %exchange_stream_2.1 = (f32[1,24,1024]{2,1,0:T(8,128)}, f32[1,24,1024]{2,1,0:T(8,128)}, f32[64,1024]{1,0:T(8,128)}) custom-call(bf16[4,1,24,1024]{3,2,1,0:T(8,128)(2,1)} %fusion.35.refs_0_, bf16[4,1,24,1024]{3,2,1,0:T(8,128)(2,1)} %dynamic-slice_bitcast_fusion.refs_1_, bf16[4,64,1024]{2,1,0:T(8,128)(2,1)} %bitcast.154), custom_call_target="tpu_custom_call" | custom-call | tf_op jit(solution)/shard_map/exchange_stream_2/pallas_call | solution.py:93
  120.2 1.7 copy-done.6
  121.9 1.8 fusion.36
  123.6 6.6 %fusion.18 = (bf16[6144,256]{0,1:T(8,128)(2,1)S(1)}, bf16[6144,256]{0,1:T(8,128)(2,1)S(1)}) fusion(f32[1,6144,512]{1,2,0:T(8,128)} %copy-done.8, bf16[6144,256]{1,0:T(8,128)(2,1)S(1)} %fusion.8, bf16[256,256]{1,0:T(8,128)(2,1)S(1)} %copy-done.21), kind=kOutput, calls=%fused_computation.37 | convolution fusion | flops 825753600 | bytes 22151168 | tf_op jit(solution)/shard_map/bsd,cd->bsc/dot_general | solution.py:22
  130.3 8.3 %fusion.59 = (bf16[1,6144,512]{2,1,0:T(8,128)(2,1)}, f32[1,6144,512]{2,1,0:T(8,128)}) fusion(bf16[512,512]{1,0:T(8,128)(2,1)S(1)} %copy-done.16, bf16[6144,256]{0,1:T(8,128)(2,1)S(1)} %get-tuple-element.44, bf16[6144,256]{0,1:T(8,128)(2,1)S(1)} %get-tuple-element.43), kind=kOutput, calls=%fused_computation.95 | convolution fusion | flops 3236954112 | bytes 25690112 | tf_op jit(solution)/shard_map/bsd,cd->bsc/dot_general | solution.py:22
  138.6 4.3 %fusion.34 = bf16[512,512]{1,0:T(8,128)(2,1)} fusion(bf16[6144,256]{0,1:T(8,128)(2,1)S(1)} %get-tuple-element.44, bf16[6144,256]{0,1:T(8,128)(2,1)S(1)} %get-tuple-element.43, bf16[1,6144,256]{2,1,0:T(8,128)(2,1)S(1)} %copy-done.3, bf16[1,5632,256]{2,1,0:T(8,128)(2,1)S(1)} %copy-done.9, bf16[1,512,256]{2,1,0:T(8,128)(2,1)S(1)} %copy-done.25), kind=kOutput, calls=%fused_computation.52 | convolution fusion | flops 3252944896 | bytes 13107200 | tf_op jit(solution)/shard_map/bsc,bsd->cd/dot_general | solution.py:22
  142.9 12.1 %exchange_stream_3.1 = (f32[128,512]{1,0:T(8,128)}, f32[64,256]{1,0:T(8,128)}) custom-call(bf16[4,128,512]{2,1,0:T(8,128)(2,1)} %bitcast.155, bf16[4,64,256]{2,1,0:T(8,128)(2,1)} %bitcast.158), custom_call_target="tpu_custom_call" | custom-call | tf_op jit(solution)/shard_map/exchange_stream_3/pallas_call | solution.py:93
  155.0 1.6 convert_element_type.187
  156.6 1.5 convert_bitcast_fusion.1.refs_1_
  158.1 10.9 %exchange_tm_4.1 = (f32[16,512]{1,0:T(8,128)}, f32[8,256]{1,0:T(8,128)}) custom-call(bf16[8,16,512]{2,1,0:T(8,128)(2,1)} %bitcast.153, bf16[8,8,256]{2,1,0:T(8,128)(2,1)} %convert_bitcast_fusion.1.refs_1_), custom_call_target="tpu_custom_call" | custom-call | tf_op jit(solution)/shard_map/exchange_tm_4/pallas_call | solution.py:93
  172.3 11.7 %exchange_tm_5.1 = (bf16[8,16,512]{2,1,0:T(8,128)(2,1)}, bf16[8,8,256]{2,1,0:T(8,128)(2,1)}, bf16[8,64,128]{2,1,0:T(8,128)(2,1)}) custom-call(bf16[16,512]{1,0:T(8,128)(2,1)} %convert_element_type.189.refs_0_, bf16[8,256]{1,0:T(8,128)(2,1)} %convert_element_type.190.refs_1_, bf16[64,128]{1,0:T(8,128)(2,1)} %dynamic-slice_convert_fusion.refs_2_), custom_call_target="tpu_custom_call" | custom-call | tf_op jit(solution)/shard_map/exchange_tm_5/pallas_call | solution.py:93
  185.3 1.6 bitcast_convert_fusion
  189.2 1.6 bitcast_add_fusion
  191.8 2.1 %slice.40 = bf16[1,5632,256]{2,1,0:T(8,128)(2,1)S(1)} slice(bf16[1,6144,512]{2,1,0:T(8,128)(2,1)} %get-tuple-element.49), slice={[0:1], [512:6144], [0:256]} | slice | bytes 5767168 | tf_op jit(solution)/shard_map/slice | solution.py:248
  196.2 9.1 %fusion.4 = bf16[1,6144,256]{2,1,0:T(8,128)(2,1)} fusion(f32[1,6144,512]{2,1,0:T(8,128)} %get-tuple-element.50, bf16[1,512,256]{2,1,0:T(8,128)(2,1)S(1)} %collective-permute-done.1, bf16[1,5632,256]{2,1,0:T(8,128)(2,1)S(1)} %slice.40, pred[6144]{0:T(1024)(128)(4,1)S(1)} %add_compare_fusion, bf16[1,6144,256]{2,1,0:T(8,128)(2,1)S(1)} %bitcast.149), kind=kLoop, calls=%fused_computation.9 | loop fusion | flops 14155776 | bytes 15734784 | tf_op jit(solution)/shard_map/convert_element_type | solution.py:249
  (75 shorter events, 22.6 us)
Async XLA Ops:
  0.6 78.6 %copy-start = (bf16[1024,768]{1,0:T(8,128)(2,1)S(1)}, bf16[1024,768]{1,0:T(8,128)(2,1)}, u32[]{:S(2)}) copy-start(bf16[1024,768]{1,0:T(8,128)(2,1)} %param.13) | copy-start | bytes 4718596
  0.6 11.6 %copy-start.16 = (bf16[512,512]{1,0:T(8,128)(2,1)S(1)}, bf16[512,512]{1,0:T(8,128)(2,1)}, u32[]{:S(2)}) copy-start(bf16[512,512]{1,0:T(8,128)(2,1)} %param.10) | copy-start | bytes 1572868
  1.8 10.5 %collective-permute-start = (bf16[1,512,256]{2,1,0:T(8,128)(2,1)S(1)}, bf16[1,512,256]{2,1,0:T(8,128)(2,1)S(1)}, u32[]{:S(2)}, u32[]{:S(2)}) collective-permute-start(bf16[1,512,256]{2,1,0:T(8,128)(2,1)S(1)} %slice.28), channel_id=1, source_target_pairs={{0,4},{4,8},{8,12},{12,16},{16,20},{20,24},{24,28},{1,5},{5,9},{9,... | collective-permute-start | bytes 786440 | tf_op jit(solution)/shard_map/ppermute | solution.py:164
  12.2 6.5 %copy-start.24 = (bf16[1,512,256]{2,1,0:T(8,128)(2,1)}, bf16[1,512,256]{2,1,0:T(8,128)(2,1)S(1)}, u32[]{:S(2)}) copy-start(bf16[1,512,256]{2,1,0:T(8,128)(2,1)S(1)} %collective-permute-done) | copy-start | bytes 786436
  18.8 5.4 %copy-start.8 = (f32[1,6144,512]{1,2,0:T(8,128)}, f32[1,6144,512]{1,2,0:T(8,128)S(1)}, u32[]{:S(2)}) copy-start(f32[1,6144,512]{1,2,0:T(8,128)S(1)} %convolution_bitcast_fusion.1) | copy-start | bytes 37748740
  18.8 5.3 %copy-start.2 = (bf16[1,6144,256]{2,1,0:T(8,128)(2,1)S(1)}, bf16[1,6144,256]{2,1,0:T(8,128)(2,1)}, u32[]{:S(2)}) copy-start(bf16[1,6144,256]{2,1,0:T(8,128)(2,1)} %param.8) | copy-start | bytes 9437188
  18.8 5.3 %copy-start.21 = (bf16[256,256]{1,0:T(8,128)(2,1)S(1)}, bf16[256,256]{1,0:T(8,128)(2,1)}, u32[]{:S(2)}) copy-start(bf16[256,256]{1,0:T(8,128)(2,1)} %param.11) | copy-start | bytes 393220
  24.1 5.3 %copy-start.4 = (bf16[6144,256]{0,1:T(8,128)(2,1)}, bf16[6144,256]{0,1:T(8,128)(2,1)S(1)}, u32[]{:S(2)}) copy-start(bf16[6144,256]{0,1:T(8,128)(2,1)S(1)} %fusion.17) | copy-start | bytes 9437188
  29.4 13.4 %copy-start.10 = (bf16[256,1024]{1,0:T(8,128)(2,1)S(1)}, bf16[256,1024]{1,0:T(8,128)(2,1)}, u32[]{:S(2)}) copy-start(bf16[256,1024]{1,0:T(8,128)(2,1)} %param.14) | copy-start | bytes 1572868
  32.7 44.5 %copy-start.11 = (bf16[256,1024]{1,0:T(8,128)(2,1)S(1)}, bf16[256,1024]{1,0:T(8,128)(2,1)}, u32[]{:S(2)}) copy-start(bf16[256,1024]{1,0:T(8,128)(2,1)} %param.12) | copy-start | bytes 1572868
  78.9 2.8 %copy-start.13 = (bf16[4,192,1024]{2,1,0:T(8,128)(2,1)}, bf16[4,192,1024]{2,1,0:T(8,128)(2,1)S(1)}, u32[]{:S(2)}) copy-start(bf16[4,192,1024]{2,1,0:T(8,128)(2,1)S(1)} %get-tuple-element.48) | copy-start | bytes 4718596
  79.3 2.5 %copy-start.12 = (bf16[4,192,1024]{2,1,0:T(8,128)(2,1)}, bf16[4,192,1024]{2,1,0:T(8,128)(2,1)S(1)}, u32[]{:S(2)}) copy-start(bf16[4,192,1024]{2,1,0:T(8,128)(2,1)S(1)} %fusion.12) | copy-start | bytes 4718596
  94.2 2.8 %copy-start.15 = (bf16[4,192,768]{2,1,0:T(8,128)(2,1)S(1)}, bf16[4,192,768]{2,1,0:T(8,128)(2,1)}, u32[]{:S(2)}) copy-start(bf16[4,192,768]{2,1,0:T(8,128)(2,1)} %get-tuple-element.31) | copy-start | bytes 3538948
  94.2 4.9 %copy-start.14 = (bf16[4,192,1024]{2,1,0:T(8,128)(2,1)S(1)}, bf16[4,192,1024]{2,1,0:T(8,128)(2,1)}, u32[]{:S(2)}) copy-start(bf16[4,192,1024]{2,1,0:T(8,128)(2,1)} %copy-done.13) | copy-start | bytes 4718596
  99.1 1.5 copy-start.23
  100.6 2.1 %copy-start.17 = (bf16[4,192,256]{2,1,0:T(8,128)(2,1)S(1)}, bf16[4,192,256]{2,1,0:T(8,128)(2,1)}, u32[]{:S(2)}) copy-start(bf16[4,192,256]{2,1,0:T(8,128)(2,1)} %get-tuple-element.30) | copy-start | bytes 1179652
  100.6 17.1 %copy-start.20 = (bf16[1,24,1024]{2,1,0:T(8,128)(2,1)S(1)}, bf16[1,24,1024]{2,1,0:T(8,128)(2,1)}, u32[]{:S(2)}) copy-start(bf16[1,24,1024]{2,1,0:T(8,128)(2,1)} %refs_1_.1) | copy-start | bytes 147460
  118.9 3.0 %copy-start.5 = (bf16[6144,256]{0,1:T(8,128)(2,1)S(1)}, bf16[6144,256]{0,1:T(8,128)(2,1)}, u32[]{:S(2)}) copy-start(bf16[6144,256]{0,1:T(8,128)(2,1)} %copy-done.4) | copy-start | bytes 9437188
  120.2 1.7 copy-start.6
  130.2 8.4 %copy-start.3 = (bf16[1,6144,256]{2,1,0:T(8,128)(2,1)S(1)}, bf16[1,6144,256]{2,1,0:T(8,128)(2,1)}, u32[]{:S(2)}) copy-start(bf16[1,6144,256]{2,1,0:T(8,128)(2,1)} %param.8) | copy-start | bytes 9437188
  130.2 8.3 %copy-start.9 = (bf16[1,5632,256]{2,1,0:T(8,128)(2,1)S(1)}, bf16[1,5632,256]{2,1,0:T(8,128)(2,1)}, u32[]{:S(2)}) copy-start(bf16[1,5632,256]{2,1,0:T(8,128)(2,1)} %slice.29) | copy-start | bytes 8650756
  130.2 8.3 %copy-start.25 = (bf16[1,512,256]{2,1,0:T(8,128)(2,1)S(1)}, bf16[1,512,256]{2,1,0:T(8,128)(2,1)}, u32[]{:S(2)}) copy-start(bf16[1,512,256]{2,1,0:T(8,128)(2,1)} %copy-done.24) | copy-start | bytes 786436
  138.6 50.6 %copy-start.18 = (f32[64,1024]{1,0:T(8,128)S(1)}, f32[64,1024]{1,0:T(8,128)}, u32[]{:S(2)}) copy-start(f32[64,1024]{1,0:T(8,128)} %get-tuple-element.41) | copy-start | bytes 786436
  142.9 48.0 %copy-start.19 = (bf16[4,8,24,128]{3,2,1,0:T(8,128)(2,1)S(1)}, bf16[4,8,24,128]{3,2,1,0:T(8,128)(2,1)}, u32[]{:S(2)}) copy-start(bf16[4,8,24,128]{3,2,1,0:T(8,128)(2,1)} %get-tuple-element.38) | copy-start | bytes 589828
  187.9 8.3 %collective-permute-start.1 = (bf16[1,512,256]{2,1,0:T(8,128)(2,1)S(1)}, bf16[1,512,256]{2,1,0:T(8,128)(2,1)S(1)}, u32[]{:S(2)}, u32[]{:S(2)}) collective-permute-start(bf16[1,512,256]{2,1,0:T(8,128)(2,1)S(1)} %slice.41), channel_id=1, source_target_pairs={{4,0},{8,4},{12,8},{16,12},{20,16},{24,20},{28,24},{5,1},{9,5},{13... | collective-permute-start | bytes 786440 | tf_op jit(solution)/shard_map/ppermute | solution.py:164
  190.9 3.1 %copy-start.22 = (f32[1,24,1024]{2,1,0:T(8,128)S(1)}, f32[1,24,1024]{2,1,0:T(8,128)}, u32[]{:S(2)}) copy-start(f32[1,24,1024]{2,1,0:T(8,128)} %get-tuple-element.32) | copy-start | bytes 294916
  191.8 4.4 %copy-start.7 = (bf16[24,256,256]{2,1,0:T(8,128)(2,1)S(1)}, bf16[24,256,256]{2,1,0:T(8,128)(2,1)}, u32[]{:S(2)}) copy-start(bf16[24,256,256]{2,1,0:T(8,128)(2,1)} %copy-done.6) | copy-start | bytes 9437188
  196.2 9.1 %copy-start.1 = (bf16[1024,768]{1,0:T(8,128)(2,1)S(1)}, bf16[1024,768]{1,0:T(8,128)(2,1)}, u32[]{:S(2)}) copy-start(bf16[1024,768]{1,0:T(8,128)(2,1)} %param.13) | copy-start | bytes 4718596

commit v2 on v1

--- a/solution.py
+++ b/solution.py
@@ -14,6 +14,7 @@
 EPS = 1e-05
 BF16 = jnp.bfloat16
 F32 = jnp.float32
+HIGH = lax.Precision.HIGHEST
 MESH = pl.DeviceIdType.MESH
 VMEM_SPEC = pl.BlockSpec(memory_space=pltpu.VMEM)
 
@@ -26,7 +27,7 @@
     k = len(kinds)
     ins, outs = refs[:k], refs[k : 2 * k]
     rest = list(refs[2 * k :])
-    slots = [rest.pop(0) if kind == "reduce" else None for kind in kinds]
+    slots = [rest.pop(0) if kind.startswith("reduce") else None for kind in kinds]
     send, recv, local_sem = rest
     me = lax.axis_index(axis)
     barrier = pltpu.get_barrier_semaphore()
@@ -41,7 +42,7 @@
         for d in range(1, n):
             peer = lax.rem(me + d, n)
             src = ins[j] if kind.startswith("gather") else ins[j].at[peer]
-            if kind == "reduce":
+            if kind.startswith("reduce"):
                 dst = slots[j].at[d - 1]
             elif kind.endswith("1"):
                 dst = outs[j].at[:, me]
@@ -57,7 +58,7 @@
             )
             copy.start()
             copies.append(copy)
-        if kind != "reduce":
+        if not kind.startswith("reduce"):
             src = ins[j] if kind.startswith("gather") else ins[j].at[me]
             dst = outs[j].at[:, me] if kind.endswith("1") else outs[j].at[me]
             copy = pltpu.make_async_copy(src, dst, local_sem.at[j])
@@ -68,11 +69,11 @@
     for copy in copies:
         copy.wait()
     for j, kind in enumerate(kinds):
-        if kind == "reduce":
+        if kind.startswith("reduce"):
             total = ins[j][me].astype(F32)
             for d in range(1, n):
                 total += slots[j][d - 1].astype(F32)
-            outs[j][...] = total
+            outs[j][...] = total.astype(outs[j].dtype)
 
 
 def exchange(axis, collective, items):
@@ -82,8 +83,8 @@
     shapes, slots = [], []
     for kind, array in items:
         inner = array.shape if kind.startswith("gather") else array.shape[1:]
-        if kind == "reduce":
-            shapes.append(jax.ShapeDtypeStruct(inner, F32))
+        if kind.startswith("reduce"):
+            shapes.append(jax.ShapeDtypeStruct(inner, BF16 if kind == "reduceb" else F32))
             slots.append(pltpu.VMEM((n - 1,) + inner, array.dtype))
         elif kind.endswith("1"):
             shapes.append(jax.ShapeDtypeStruct((inner[0], n) + inner[1:], array.dtype))
@@ -158,6 +159,153 @@
     )(group_len, proj, d_context)
 
 
+def tile_valid(info_ref, tile, step):
+    row = lax.broadcasted_iota(jnp.int32, (tile, 1), 0)
+    return info_ref[0] + step * tile + row < info_ref[1]
+
+
+def joined_tile(first, in_ref, past_ref, cur_ref):
+    past = jnp.where(first, in_ref[...], past_ref[...])
+    return jnp.concatenate([past, cur_ref[...]], axis=1)
+
+
+def forward_kernel(info_ref, in_ref, past_ref, cur_ref, w_ref, t_ref, s_ref, hs_ref, ss_ref):
+    i = pl.program_id(0)
+    tile, chans = cur_ref.shape
+    joined = joined_tile(i == 0, in_ref, past_ref, cur_ref)
+    mixed = jnp.dot(joined, w_ref[...], preferred_element_type=F32)
+    t = jnp.tanh(mixed[:, :chans])
+    s = jax.nn.sigmoid(mixed[:, chans:])
+    t_ref[...] = t
+    s_ref[...] = s
+    valid = tile_valid(info_ref, tile, i)
+    hidden = jnp.where(valid, (t * s).astype(BF16).astype(F32), 0.0)
+    kept = jnp.where(valid, cur_ref[...].astype(F32), 0.0)
+    for j in range(tile // POOL):
+        rows = slice(j * POOL, (j + 1) * POOL)
+        hs_ref[0, j : j + 1, :] = jnp.sum(hidden[rows], axis=0, keepdims=True)
+        ss_ref[0, j : j + 1, :] = jnp.sum(kept[rows], axis=0, keepdims=True)
+
+
+def backward_kernel(
+    steps, info_ref, in_ref, past_ref, cur_ref, t_ref, s_ref, dh_ref, dr_ref, w_ref,
+    sig_ref, first_ref, g_ref, acc_ref, later_ref,
+):
+    i = pl.program_id(0)
+    step = steps - 1 - i
+    tile, chans = cur_ref.shape
+
+    @pl.when(i == 0)
+    def _():
+        acc_ref[...] = jnp.zeros_like(acc_ref)
+        later_ref[...] = jnp.zeros_like(later_ref)
+
+    joined = joined_tile(step == 0, in_ref, past_ref, cur_ref)
+    valid = tile_valid(info_ref, tile, step)
+
+    def spread(ref):
+        pieces = [
+            jnp.broadcast_to(ref[0, j : j + 1, :], (POOL, chans)) for j in range(tile // POOL)
+        ]
+        return jnp.where(valid, jnp.concatenate(pieces, axis=0), 0.0)
+
+    t, s = t_ref[...], s_ref[...]
+    d_hidden = spread(dh_ref)
+    d_gate = d_hidden * s
+    d_mixed = jnp.concatenate(
+        [d_gate * (1.0 - t * t), d_gate * t * (1.0 - s)], axis=1
+    ).astype(BF16)
+    acc_ref[...] += lax.dot_general(
+        joined, d_mixed, (((0,), (0,)), ((), ())), preferred_element_type=F32
+    )
+    d_joined = lax.dot_general(
+        d_mixed, w_ref[...], (((1,), (1,)), ((), ())), preferred_element_type=F32
+    )
+    sig_ref[...] = (spread(dr_ref) + d_joined[:, chans:] + later_ref[...].astype(F32)).astype(BF16)
+    later_ref[...] = d_joined[:, :chans].astype(BF16)
+
+    @pl.when(i == steps - 1)
+    def _():
+        first_ref[...] = d_joined[:, :chans].astype(BF16)
+        g_ref[...] = acc_ref[...].astype(BF16)
+
+
+def add_kernel(sig_ref, extra_ref, out_ref):
+    out_ref[...] = (sig_ref[...].astype(F32) + extra_ref[...].astype(F32)).astype(BF16)
+
+
+def add_last(d_sig, arriving):
+    samples, chans = d_sig.shape
+    rows = arriving.shape[0]
+    last = pl.BlockSpec((rows, chans), lambda i: (samples // rows - 1, 0))
+    return pl.pallas_call(
+        add_kernel,
+        grid=(1,),
+        out_shape=jax.ShapeDtypeStruct(d_sig.shape, BF16),
+        in_specs=[last, pl.BlockSpec((rows, chans), lambda i: (0, 0))],
+        out_specs=last,
+        input_output_aliases={0: 0},
+        name="add_last",
+    )(d_sig, arriving)
+
+
+def conv_forward(info, incoming, signal, w_conv):
+    samples, chans = signal.shape
+    tile = DILATION_STEP
+    steps, pools = samples // tile, tile // POOL
+    block = pl.BlockSpec((tile, chans), lambda i: (i, 0))
+    sums = pl.BlockSpec((1, pools, chans), lambda i: (i, 0, 0))
+    gate = jax.ShapeDtypeStruct((samples, chans), F32)
+    pooled = jax.ShapeDtypeStruct((steps, pools, chans), F32)
+    return pl.pallas_call(
+        forward_kernel,
+        grid=(steps,),
+        out_shape=(gate, gate, pooled, pooled),
+        in_specs=[
+            pl.BlockSpec(memory_space=pltpu.SMEM),
+            pl.BlockSpec((tile, chans), lambda i: (0, 0)),
+            pl.BlockSpec((tile, chans), lambda i: (jnp.maximum(i - 1, 0), 0)),
+            block,
+            pl.BlockSpec(w_conv.shape, lambda i: (0, 0)),
+        ],
+        out_specs=(block, block, sums, sums),
+        name="conv_forward",
+    )(info, incoming, signal, signal, w_conv)
+
+
+def conv_backward(info, incoming, signal, t, s, d_hidden, d_resid, w_conv):
+    samples, chans = signal.shape
+    tile = DILATION_STEP
+    steps, pools = samples // tile, tile // POOL
+    block = pl.BlockSpec((tile, chans), lambda i: (steps - 1 - i, 0))
+    fixed = pl.BlockSpec((tile, chans), lambda i: (0, 0))
+    sums = pl.BlockSpec((1, pools, chans), lambda i: (steps - 1 - i, 0, 0))
+    whole = pl.BlockSpec(w_conv.shape, lambda i: (0, 0))
+    return pl.pallas_call(
+        functools.partial(backward_kernel, steps),
+        grid=(steps,),
+        out_shape=(
+            jax.ShapeDtypeStruct((samples, chans), BF16),
+            jax.ShapeDtypeStruct((tile, chans), BF16),
+            jax.ShapeDtypeStruct(w_conv.shape, BF16),
+        ),
+        in_specs=[
+            pl.BlockSpec(memory_space=pltpu.SMEM),
+            fixed,
+            pl.BlockSpec((tile, chans), lambda i: (jnp.maximum(steps - 2 - i, 0), 0)),
+            block,
+            block,
+            block,
+            sums,
+            sums,
+            whole,
+        ],
+        out_specs=(block, fixed, whole),
+        scratch_shapes=[pltpu.VMEM(w_conv.shape, F32), pltpu.VMEM((tile, chans), BF16)],
+        name="conv_backward",
+    )(info, incoming, signal, signal, t, s, d_hidden, d_resid, w_conv)
+
+
 def shifted(value, axis, by):
     length = lax.axis_size(axis)
     pairs = [(i, i + by) for i in range(length) if 0 <= i + by < length]
@@ -174,17 +322,13 @@
     tm = lax.axis_index("tm")
     group = stays * parts
     total = toks * tms
-    incoming = shifted(signal[:, samples - DILATION_STEP :], "tm", 1)
-    past = jnp.concatenate([incoming, signal[:, : samples - DILATION_STEP]], axis=1)
-    joined = jnp.concatenate([past, signal], axis=2)
-    mixed = dot("bsc,cd->bsd", joined, w_conv)
-    tanh_f = jnp.tanh(mixed[..., :chans])
-    sig_g = jax.nn.sigmoid(mixed[..., chans:])
-    hidden = (tanh_f * sig_g).astype(BF16)
-    pos = tm * samples + jnp.arange(samples, dtype=jnp.int32)
-    valid = (pos[None, :] < lengths[:, None])[..., None]
-    resid = jnp.where(valid, signal.astype(F32) + dot("bsc,cd->bsd", hidden, w_res), 0.0)
-    pooled = jnp.mean(resid.reshape(stays, toks, POOL, chans), axis=2).astype(BF16)
+    flat = signal.reshape(samples, chans)
+    incoming = shifted(flat[samples - DILATION_STEP :], "tm", 1)
+    info = jnp.stack([tm * samples, lengths[0]]).astype(jnp.int32)
+    tanh_f, sig_g, h_sum, s_sum = conv_forward(info, incoming, flat, w_conv)
+    h_sum = h_sum.reshape(toks, chans)
+    h_part = jnp.dot(h_sum, w_res.astype(F32), precision=HIGH)
+    pooled = ((s_sum.reshape(toks, chans) + h_part) / POOL).astype(BF16)[None]
     own_tok = dot("btc,cd->btd", pooled, w_in).astype(BF16)
     lens8 = jnp.broadcast_to(lengths.reshape(stays, 1, 1), (stays, 8, 128))
     g_pool, g_dout, g_len = exchange(
@@ -233,42 +377,46 @@
     out = (own_tok.astype(F32) + s_out).astype(BF16)
     d_tok = (s_group + d_out.astype(F32)).astype(BF16)
     d_pooled = dot("btd,cd->btc", d_tok, w_in)
-    spread = jnp.repeat(d_pooled / POOL, POOL, axis=1)
-    d_resid = jnp.where(valid, spread, 0.0).astype(BF16)
-    g_res = dot("bsc,bsd->cd", hidden, d_resid)
-    d_hidden = dot("bsd,cd->bsc", d_resid, w_res)
-    d_mixed = jnp.concatenate(
-        [d_hidden * (1.0 - tanh_f * tanh_f) * sig_g, d_hidden * tanh_f * sig_g * (1.0 - sig_g)],
-        axis=2,
-    ).astype(BF16)
-    g_conv = dot("bsc,bsd->cd", joined, d_mixed)
-    d_joined = dot("bsd,cd->bsc", d_mixed, w_conv)
-    past_grad = d_joined[..., :chans].astype(BF16)
-    arriving = shifted(past_grad[:, :DILATION_STEP], "tm", -1)
-    later = jnp.concatenate([past_grad[:, DILATION_STEP:], arriving], axis=1)
-    d_signal = (d_resid.astype(F32) + d_joined[..., chans:] + later.astype(F32)).astype(BF16)
+    d_res16 = (d_pooled / POOL).astype(BF16).reshape(toks, chans)
+    g_res = lax.dot_general(h_sum, d_res16.astype(F32), (((0,), (0,)), ((), ())), precision=HIGH)
+    d_hidden = lax.dot_general(
+        d_res16, w_res, (((1,), (1,)), ((), ())), preferred_element_type=F32
+    )
+    per_tile = (samples // DILATION_STEP, DILATION_STEP // POOL, chans)
+    d_sig, first, g_conv = conv_backward(
+        info,
+        incoming,
+        flat,
+        tanh_f,
+        sig_g,
+        d_hidden.reshape(per_tile),
+        d_res16.astype(F32).reshape(per_tile),
+        w_conv,
+    )
+    arriving = shifted(first, "tm", -1)
+    d_signal = add_last(d_sig, arriving)[None]
     s_conv, s_res = exchange(
         "stream",
         3,
         [
-            ("reduce", g_conv.astype(BF16).reshape(parts, -1, 2 * chans)),
-            ("reduce", g_res.astype(BF16).reshape(parts, -1, chans)),
+            ("reduceb", g_conv.reshape(parts, -1, 2 * chans)),
+            ("reduceb", g_res.astype(BF16).reshape(parts, -1, chans)),
         ],
     )
     t_conv, t_res = exchange(
         "tm",
         4,
         [
-            ("reduce", s_conv.astype(BF16).reshape(tms, -1, 2 * chans)),
-            ("reduce", s_res.astype(BF16).reshape(tms, -1, chans)),
+            ("reduceb", s_conv.reshape(tms, -1, 2 * chans)),
+            ("reduceb", s_res.reshape(tms, -1, chans)),
         ],
     )
     a_conv, a_res, a_in = exchange(
         "tm",
         5,
         [
-            ("gather", t_conv.astype(BF16)),
-            ("gather", t_res.astype(BF16)),
+            ("gather", t_conv),
+            ("gather", t_res),
             ("gather", g_in_cols.astype(BF16)),
         ],
     )

time: 206 us -> 186 us (0.903)
  Pallas kernels: 98.3 us -> 130 us
  matrix products: 50.1 us -> 19.5 us
  other arithmetic: 28.7 us -> 8.36 us
  local copies, waits for them, and re-layouts: 17.6 us -> 10.5 us
  waiting for transfers between devices: 2.66 us -> 8.02 us
    dot_general x17 -> x11, matrix products: 50.1 us -> 18.2 us  [dot(): return jnp.einsum(eq, a, b, preferred_element_type=F32)]
    pallas_call x0 -> x3, Pallas kernels: none -> 31.6 us  [the longest x1 16.6 us: conv_backward(): pl.pallas_call(functools.partial(backward_kernel, steps), grid=(steps,),...]
    convert_element_type x6 -> x2, other arithmetic: 15 us -> 1.26 us  [the longest x1 0.64 us: local(): pooled = ((s_sum.reshape(toks, chans) + h_part) / POOL).astype(BF16)[None]]
    slice x4 -> x1, local copies, waits for them, and re-layouts: 7.81 us -> 1.09 us  [local(): incoming = shifted(flat[samples - DILATION_STEP:], 'tm', 1)]
    ppermute x2, waiting for transfers between devices: 2.66 us -> 8.02 us  [shifted(): return lax.ppermute(value, axis, pairs)]
    reduce_sum x1 -> x0, other arithmetic: 3.28 us -> none  [local(): jnp.mean(resid.reshape(stays, toks, POOL, chans), axis=2).astype(BF16)]
    unnamed x53 -> x37, local copies, waits for them, and re-layouts: 5.56 us -> 3.21 us
  transfers between devices with their start and end apart: 2 -> 2, of which waited for: 2 -> 2; matrix products, arithmetic and copies ran while one was open for 4% -> 2% of each run, Pallas kernels for 0% -> 0%
where the time goes in v2:
time: 186 us; the launch traced here: 184 us
  Pallas kernels  130 us (70%)
  matrix products  19.5 us (10%)
  local copies, waits for them, and re-layouts  10.5 us (6%)
  other arithmetic  8.36 us (4%)
  waiting for transfers between devices  8.02 us (4%)
  starting transfers between devices  6.2 us (3%)
    pallas_call x6, Pallas kernels, exchange(): pl.pallas_call(functools.partial(exchange_kernel, axis, n, kinds), out_sh...  85.8 us
    dot_general x11, matrix products, dot(): return jnp.einsum(eq, a, b, preferred_element_type=F32)  18.2 us
    pallas_call x1, Pallas kernels, conv_backward(): pl.pallas_call(functools.partial(backward_kernel, steps), grid=(steps,),...  16.6 us
    pallas_call x1, Pallas kernels, conv_forward(): pl.pallas_call(forward_kernel, grid=(steps,), out_shape=(gate, gate, pool...  13.2 us
    pallas_call x1, Pallas kernels, attention(): pl.pallas_call(functools.partial(attention_kernel, heads, size, 1.0 / mat...  12.5 us
    ppermute x2, waiting for transfers between devices, shifted(): return lax.ppermute(value, axis, pairs)  8.02 us
    ppermute x2, starting transfers between devices, shifted(): return lax.ppermute(value, axis, pairs)  6.2 us
  transfers between devices with their start and end apart: 2, of which 2 were waited for; matrix products, arithmetic and copies ran while one was open for 2% of the time, Pallas kernels for 0%

profile of v2, /device:TPU:0, one launch (start us, length us, event | category | flops | bytes accessed | tf_op | source)
XLA Modules:
  0.0 184.1 jit_solution(18393180128484657950)
XLA Ops:
  0.6 1.1 slice_bitcast_fusion
  1.7 4.9 %collective-permute-start = (bf16[512,256]{1,0:T(8,128)(2,1)S(1)}, bf16[512,256]{1,0:T(8,128)(2,1)S(1)}, u32[]{:S(2)}, u32[]{:S(2)}) collective-permute-start(bf16[512,256]{1,0:T(8,128)(2,1)S(1)} %slice_bitcast_fusion), channel_id=1, source_target_pairs={{0,4},{4,8},{8,12},{12,16},{16,20},{20,24},{24,28},{1,5},{5,9},{9,... | collective-permute-start | bytes 786440 | tf_op jit(solution)/shard_map/ppermute | solution.py:312
  7.9 4.3 %collective-permute-done.in_ref = bf16[512,256]{1,0:T(8,128)(2,1)S(1)} collective-permute-done((bf16[512,256]{1,0:T(8,128)(2,1)S(1)}, bf16[512,256]{1,0:T(8,128)(2,1)S(1)}, u32[]{:S(2)}, u32[]{:S(2)}) %collective-permute-start) | collective-permute-done | bytes 262176 | tf_op jit(solution)/shard_map/ppermute | solution.py:312
  12.9 13.2 %conv_forward.1 = (f32[6144,256]{1,0:T(8,128)}, f32[6144,256]{1,0:T(8,128)}, f32[12,2,256]{2,1,0:T(2,128)}, f32[12,2,256]{2,1,0:T(2,128)}) custom-call(s32[2]{0:T(128)} %pad_add_fusion.info_ref, bf16[512,256]{1,0:T(8,128)(2,1)} %copy-done.7, bf16[6144,256]{1,0:T(8,128)(2,1)} %bitcast.106, bf16[6144,256]{1,0:T(8,128)(2,1)} %bitcast.107, bf16[512,512]{1,0:T(8,128)(2,1)} %w_ref.3), custom_call_target="tpu_custom_call" | custom-call | tf_op jit(solution)/shard_map/conv_forward/pallas_call | solution.py:260
  29.1 7.5 %exchange_stream_0.1 = (bf16[4,1,24,256]{3,2,1,0:T(8,128)(2,1)}, bf16[4,1,24,1024]{3,2,1,0:T(8,128)(2,1)}, s32[4,1,8,128]{3,2,1,0:T(8,128)}) custom-call(bf16[1,24,256]{2,1,0:T(8,128)(2,1)} %bitcast.120, bf16[1,24,1024]{2,1,0:T(8,128)(2,1)} %refs_1_.1, s32[1,8,128]{2,1,0:T(8,128)} %broadcast_in_dim.17.refs_2_), custom_call_target="tpu_custom_call" | custom-call | tf_op jit(solution)/shard_map/exchange_stream_0/pallas_call | solution.py:94
  36.6 1.4 slice_reduce_fusion.len_ref
  38.0 1.8 %convolution_convert_fusion.3.refs_1_ = bf16[4,24,256]{2,1,0:T(8,128)(2,1)} fusion(bf16[256,1024]{1,0:T(8,128)(2,1)S(1)} %copy-done.1, bf16[4,1,24,1024]{3,2,1,0:T(8,128)(2,1)} %get-tuple-element.36), kind=kOutput, calls=%fused_computation.26 | convolution fusion | flops 50356224 | bytes 770048 | tf_op jit(solution)/shard_map/btd,ed->bte/dot_general | solution.py:23
  39.9 1.0 copy.24
  41.5 29.6 %exchange_tm_1.1 = (bf16[4,8,24,256]{3,2,1,0:T(8,128)(2,1)}, bf16[4,8,24,256]{3,2,1,0:T(8,128)(2,1)}, bf16[4,8,24,128]{3,2,1,0:T(8,128)(2,1)}) custom-call(bf16[4,24,256]{2,1,0:T(8,128)(2,1)} %bitcast.121, bf16[4,24,256]{2,1,0:T(8,128)(2,1)} %convolution_convert_fusion.3.refs_1_, bf16[8,4,24,128]{3,2,1,0:T(8,128)(2,1)} %bitcast.111), custom_call_target="tpu_custom_call" | custom-call | tf_op jit(solution)/shard_map/exchange_tm_1/pallas_call | solution.py:94
  71.2 1.7 fusion.1
  74.0 2.4 %fusion.12.proj_ref = bf16[4,192,768]{2,1,0:T(8,128)(2,1)} fusion(bf16[4,192,1024]{2,1,0:T(8,128)(2,1)S(1)} %fusion.2, bf16[1024,768]{1,0:T(8,128)(2,1)S(1)} %copy-done), kind=kOutput, calls=%fused_computation.17 | convolution fusion | flops 1208549376 | bytes 4325376 | tf_op jit(solution)/shard_map/btd,de->bte/dot_general | solution.py:23
  76.4 12.5 %attention.1 = (bf16[4,192,256]{2,1,0:T(8,128)(2,1)}, bf16[4,192,768]{2,1,0:T(8,128)(2,1)}) custom-call(s32[4]{0:T(128)} %slice_reduce_fusion.len_ref, bf16[4,192,768]{2,1,0:T(8,128)(2,1)} %fusion.12.proj_ref, bf16[4,192,256]{2,1,0:T(8,128)(2,1)} %bitcast.117), custom_call_target="tpu_custom_call" | custom-call | tf_op jit(solution)/shard_map/attention/pallas_call | solution.py:149
  88.9 2.8 %fusion.8 = f32[4,192,1024]{2,1,0:T(8,128)S(1)} fusion(bf16[4,192,768]{2,1,0:T(8,128)(2,1)} %get-tuple-element.40, bf16[1024,768]{1,0:T(8,128)(2,1)S(1)} %copy-done), kind=kOutput, calls=%fused_computation.13 | convolution fusion | flops 1207959552 | bytes 5898240 | tf_op jit(solution)/shard_map/bte,de->btd/dot_general | solution.py:23
  91.7 1.5 fusion.6
  93.2 1.4 fusion.15
  95.3 1.7 fusion.16.refs_0_
  97.0 14.1 %exchange_stream_2.1 = (f32[1,24,1024]{2,1,0:T(8,128)}, f32[1,24,1024]{2,1,0:T(8,128)}, f32[64,1024]{1,0:T(8,128)}) custom-call(bf16[4,1,24,1024]{3,2,1,0:T(8,128)(2,1)} %fusion.16.refs_0_, bf16[4,1,24,1024]{3,2,1,0:T(8,128)(2,1)} %dynamic-slice_bitcast_fusion.refs_1_, bf16[4,64,1024]{2,1,0:T(8,128)(2,1)} %bitcast.115), custom_call_target="tpu_custom_call" | custom-call | tf_op jit(solution)/shard_map/exchange_stream_2/pallas_call | solution.py:94
  111.1 1.2 fusion.21
  113.1 1.0 convolution_convert_fusion.2
  114.2 1.3 convolution_bitcast_fusion.3
  115.5 2.0 %convolution_bitcast_fusion.1 = f32[128,768]{1,0:T(8,128)} fusion(bf16[4,192,768]{2,1,0:T(8,128)(2,1)S(1)} %copy-done.6, bf16[4,192,1024]{2,1,0:T(8,128)(2,1)} %copy-done.3, s32[]{:T(128)S(6)} %select_n.12), kind=kOutput, calls=%fused_computation.20 | convolution fusion | flops 150994944 | bytes 1769476 | tf_op jit(solution)/shard_map/btd,bte->de/dot_general | solution.py:23
  118.8 16.6 %conv_backward.1 = (bf16[6144,256]{1,0:T(8,128)(2,1)}, bf16[512,256]{1,0:T(8,128)(2,1)}, bf16[512,512]{1,0:T(8,128)(2,1)}) custom-call(s32[2]{0:T(128)} %pad_add_fusion.info_ref, bf16[512,256]{1,0:T(8,128)(2,1)} %copy-done.7, bf16[6144,256]{1,0:T(8,128)(2,1)} %bitcast.108, bf16[6144,256]{1,0:T(8,128)(2,1)} %bitcast.109, ...), custom_call_target="tpu_custom_call" | custom-call | tf_op jit(solution)/shard_map/conv_backward/pallas_call | solution.py:284
  135.4 12.0 %exchange_stream_3.1 = (bf16[128,512]{1,0:T(8,128)(2,1)}, bf16[64,256]{1,0:T(8,128)(2,1)}) custom-call(bf16[4,128,512]{2,1,0:T(8,128)(2,1)} %bitcast.114, bf16[4,64,256]{2,1,0:T(8,128)(2,1)} %bitcast.116), custom_call_target="tpu_custom_call" | custom-call | tf_op jit(solution)/shard_map/exchange_stream_3/pallas_call | solution.py:94
  147.5 10.9 %exchange_tm_4.1 = (bf16[16,512]{1,0:T(8,128)(2,1)}, bf16[8,256]{1,0:T(8,128)(2,1)}) custom-call(bf16[8,16,512]{2,1,0:T(8,128)(2,1)} %bitcast.119, bf16[8,8,256]{2,1,0:T(8,128)(2,1)} %bitcast.122), custom_call_target="tpu_custom_call" | custom-call | tf_op jit(solution)/shard_map/exchange_tm_4/pallas_call | solution.py:94
  158.4 11.7 %exchange_tm_5.1 = (bf16[8,16,512]{2,1,0:T(8,128)(2,1)}, bf16[8,8,256]{2,1,0:T(8,128)(2,1)}, bf16[8,64,128]{2,1,0:T(8,128)(2,1)}) custom-call(bf16[16,512]{1,0:T(8,128)(2,1)} %get-tuple-element.50.refs_0_, bf16[8,256]{1,0:T(8,128)(2,1)} %get-tuple-element.51.refs_1_, bf16[64,128]{1,0:T(8,128)(2,1)} %dynamic-slice_convert_fusion.refs_2_), custom_call_target="tpu_custom_call" | custom-call | tf_op jit(solution)/shard_map/exchange_tm_5/pallas_call | solution.py:94
  170.1 1.4 bitcast_convert_fusion.1
  171.5 1.6 bitcast_convert_fusion
  173.1 1.3 collective-permute-start.1
  174.4 1.6 bitcast_add_fusion
  176.1 1.0 convolution_bitcast_fusion.2
  177.9 3.7 %collective-permute-done.1.extra_ref = bf16[512,256]{1,0:T(8,128)(2,1)S(1)} collective-permute-done((bf16[512,256]{1,0:T(8,128)(2,1)}, bf16[512,256]{1,0:T(8,128)(2,1)S(1)}, u32[]{:S(2)}, u32[]{:S(2)}) %collective-permute-start.1) | collective-permute-done | bytes 262176 | tf_op jit(solution)/shard_map/ppermute | solution.py:312
  182.3 1.8 add_last.1
  (52 shorter events, 10.4 us)
Async XLA Ops:
  0.6 73.3 %copy-start = (bf16[1024,768]{1,0:T(8,128)(2,1)S(1)}, bf16[1024,768]{1,0:T(8,128)(2,1)}, u32[]{:S(2)}) copy-start(bf16[1024,768]{1,0:T(8,128)(2,1)} %param.13) | copy-start | bytes 4718596
  1.7 10.5 %collective-permute-start = (bf16[512,256]{1,0:T(8,128)(2,1)S(1)}, bf16[512,256]{1,0:T(8,128)(2,1)S(1)}, u32[]{:S(2)}, u32[]{:S(2)}) collective-permute-start(bf16[512,256]{1,0:T(8,128)(2,1)S(1)} %slice_bitcast_fusion), channel_id=1, source_target_pairs={{0,4},{4,8},{8,12},{12,16},{16,20},{20,24},{24,28},{1,5},{5,9},{9,... | collective-permute-start | bytes 786440 | tf_op jit(solution)/shard_map/ppermute | solution.py:312
  12.2 0.7 copy-start.7
  12.9 14.8 %copy-start.8 = (bf16[256,256]{1,0:T(8,128)(2,1)S(1)}, bf16[256,256]{1,0:T(8,128)(2,1)}, u32[]{:S(2)}) copy-start(bf16[256,256]{1,0:T(8,128)(2,1)} %param.11) | copy-start | bytes 393220
  12.9 25.1 %copy-start.1 = (bf16[256,1024]{1,0:T(8,128)(2,1)S(1)}, bf16[256,1024]{1,0:T(8,128)(2,1)}, u32[]{:S(2)}) copy-start(bf16[256,1024]{1,0:T(8,128)(2,1)} %param.14) | copy-start | bytes 1572868
  26.1 45.0 %copy-start.2 = (bf16[256,1024]{1,0:T(8,128)(2,1)S(1)}, bf16[256,1024]{1,0:T(8,128)(2,1)}, u32[]{:S(2)}) copy-start(bf16[256,1024]{1,0:T(8,128)(2,1)} %param.12) | copy-start | bytes 1572868
  72.8 1.1 copy-start.4
  74.0 2.4 %copy-start.3 = (bf16[4,192,1024]{2,1,0:T(8,128)(2,1)}, bf16[4,192,1024]{2,1,0:T(8,128)(2,1)S(1)}, u32[]{:S(2)}) copy-start(bf16[4,192,1024]{2,1,0:T(8,128)(2,1)S(1)} %fusion.2) | copy-start | bytes 4718596
  88.9 2.8 %copy-start.5 = (bf16[4,192,1024]{2,1,0:T(8,128)(2,1)S(1)}, bf16[4,192,1024]{2,1,0:T(8,128)(2,1)}, u32[]{:S(2)}) copy-start(bf16[4,192,1024]{2,1,0:T(8,128)(2,1)} %copy-done.4) | copy-start | bytes 4718596
  91.7 1.5 copy-start.17
  94.6 16.5 %copy-start.14 = (bf16[1,24,1024]{2,1,0:T(8,128)(2,1)S(1)}, bf16[1,24,1024]{2,1,0:T(8,128)(2,1)}, u32[]{:S(2)}) copy-start(bf16[1,24,1024]{2,1,0:T(8,128)(2,1)} %refs_1_.1) | copy-start | bytes 147460
  94.6 18.4 %copy-start.9 = (bf16[256,256]{1,0:T(8,128)(2,1)S(1)}, bf16[256,256]{1,0:T(8,128)(2,1)}, u32[]{:S(2)}) copy-start(bf16[256,256]{1,0:T(8,128)(2,1)} %param.11) | copy-start | bytes 393220
  111.1 4.4 %copy-start.6 = (bf16[4,192,768]{2,1,0:T(8,128)(2,1)S(1)}, bf16[4,192,768]{2,1,0:T(8,128)(2,1)}, u32[]{:S(2)}) copy-start(bf16[4,192,768]{2,1,0:T(8,128)(2,1)} %get-tuple-element.40) | copy-start | bytes 3538948
  118.8 55.6 %copy-start.12 = (f32[64,1024]{1,0:T(8,128)S(1)}, f32[64,1024]{1,0:T(8,128)}, u32[]{:S(2)}) copy-start(f32[64,1024]{1,0:T(8,128)} %get-tuple-element.55) | copy-start | bytes 786436
  135.4 40.7 %copy-start.10 = (bf16[4,192,256]{2,1,0:T(8,128)(2,1)S(1)}, bf16[4,192,256]{2,1,0:T(8,128)(2,1)}, u32[]{:S(2)}) copy-start(bf16[4,192,256]{2,1,0:T(8,128)(2,1)} %get-tuple-element.39) | copy-start | bytes 1179652
  135.4 40.7 %copy-start.13 = (bf16[4,8,24,128]{3,2,1,0:T(8,128)(2,1)S(1)}, bf16[4,8,24,128]{3,2,1,0:T(8,128)(2,1)}, u32[]{:S(2)}) copy-start(bf16[4,8,24,128]{3,2,1,0:T(8,128)(2,1)} %get-tuple-element.52) | copy-start | bytes 589828
  135.4 41.6 %copy-start.15 = (bf16[24,256]{1,0:T(8,128)(2,1)S(1)}, bf16[24,256]{1,0:T(8,128)(2,1)}, u32[]{:S(2)}) copy-start(bf16[24,256]{1,0:T(8,128)(2,1)} %multiply_convert_fusion) | copy-start | bytes 36868
  135.4 41.6 %copy-start.16 = (f32[1,24,1024]{2,1,0:T(8,128)S(1)}, f32[1,24,1024]{2,1,0:T(8,128)}, u32[]{:S(2)}) copy-start(f32[1,24,1024]{2,1,0:T(8,128)} %get-tuple-element.41) | copy-start | bytes 294916
  173.1 8.5 %collective-permute-start.1 = (bf16[512,256]{1,0:T(8,128)(2,1)}, bf16[512,256]{1,0:T(8,128)(2,1)S(1)}, u32[]{:S(2)}, u32[]{:S(2)}) collective-permute-start(bf16[512,256]{1,0:T(8,128)(2,1)} %get-tuple-element.46), channel_id=1, source_target_pairs={{4,0},{8,4},{12,8},{16,12},{20,16},{24,20},{28,24},{5,1},{9,5},{13... | collective-permute-start | bytes 786440 | tf_op jit(solution)/shard_map/ppermute | solution.py:312
  181.6 0.7 copy-start.11

commit v3 on v2

--- a/solution.py
+++ b/solution.py
@@ -27,7 +27,7 @@
     k = len(kinds)
     ins, outs = refs[:k], refs[k : 2 * k]
     rest = list(refs[2 * k :])
-    slots = [rest.pop(0) if kind.startswith("reduce") else None for kind in kinds]
+    slots = [rest.pop(0) if kind.startswith("reduce") or kind == "gatherf" else None for kind in kinds]
     send, recv, local_sem = rest
     me = lax.axis_index(axis)
     barrier = pltpu.get_barrier_semaphore()
@@ -44,6 +44,8 @@
             src = ins[j] if kind.startswith("gather") else ins[j].at[peer]
             if kind.startswith("reduce"):
                 dst = slots[j].at[d - 1]
+            elif kind == "gatherf":
+                dst = slots[j].at[me]
             elif kind.endswith("1"):
                 dst = outs[j].at[:, me]
             else:
@@ -60,7 +62,8 @@
             copies.append(copy)
         if not kind.startswith("reduce"):
             src = ins[j] if kind.startswith("gather") else ins[j].at[me]
-            dst = outs[j].at[:, me] if kind.endswith("1") else outs[j].at[me]
+            land = slots[j] if kind == "gatherf" else outs[j]
+            dst = land.at[:, me] if kind.endswith("1") else land.at[me]
             copy = pltpu.make_async_copy(src, dst, local_sem.at[j])
             copy.start()
             locals_.append(copy)
@@ -74,6 +77,8 @@
             for d in range(1, n):
                 total += slots[j][d - 1].astype(F32)
             outs[j][...] = total.astype(outs[j].dtype)
+        elif kind == "gatherf":
+            outs[j][...] = slots[j][...].astype(F32)
 
 
 def exchange(axis, collective, items):
@@ -86,6 +91,9 @@
         if kind.startswith("reduce"):
             shapes.append(jax.ShapeDtypeStruct(inner, BF16 if kind == "reduceb" else F32))
             slots.append(pltpu.VMEM((n - 1,) + inner, array.dtype))
+        elif kind == "gatherf":
+            shapes.append(jax.ShapeDtypeStruct((n,) + inner, F32))
+            slots.append(pltpu.VMEM((n,) + inner, array.dtype))
         elif kind.endswith("1"):
             shapes.append(jax.ShapeDtypeStruct((inner[0], n) + inner[1:], array.dtype))
         else:
@@ -159,6 +167,79 @@
     )(group_len, proj, d_context)
 
 
+def riding_copies(axis, kinds, ins, slots, send, recv, keep):
+    n = lax.axis_size(axis)
+    me = lax.axis_index(axis)
+    copies = []
+    for j, kind in enumerate(kinds):
+        for d in range(1, n):
+            peer = lax.rem(me + d, n)
+            copies.append(
+                pltpu.make_async_remote_copy(
+                    src_ref=ins[j] if kind == "gather1" else ins[j].at[peer],
+                    dst_ref=slots[j].at[d - 1] if kind == "reduce" else slots[j].at[:, me],
+                    send_sem=send.at[j, d - 1],
+                    recv_sem=recv.at[j, d - 1],
+                    device_id={axis: peer},
+                    device_id_type=MESH,
+                )
+            )
+        if kind != "reduce":
+            src = ins[j] if kind == "gather1" else ins[j].at[me]
+            copies.append(pltpu.make_async_copy(src, slots[j].at[:, me], keep.at[j]))
+    return copies
+
+
+def ride_start(axis, kinds, ins, slots, send, recv, keep):
+    n = lax.axis_size(axis)
+    me = lax.axis_index(axis)
+    barrier = pltpu.get_barrier_semaphore()
+    for d in range(1, n):
+        pl.semaphore_signal(
+            barrier, inc=1, device_id={axis: lax.rem(me + d, n)}, device_id_type=MESH
+        )
+    pl.semaphore_wait(barrier, n - 1)
+    for copy in riding_copies(axis, kinds, ins, slots, send, recv, keep):
+        copy.start()
+
+
+def ride_finish(axis, kinds, ins, outs, slots, send, recv, keep):
+    n = lax.axis_size(axis)
+    me = lax.axis_index(axis)
+    for copy in riding_copies(axis, kinds, ins, slots, send, recv, keep):
+        copy.wait()
+    for j, kind in enumerate(kinds):
+        if kind == "reduce":
+            sum_ = ins[j][me].astype(F32)
+            for d in range(1, n):
+                sum_ += slots[j][d - 1].astype(F32)
+            outs[j][...] = sum_
+        else:
+            outs[j][...] = slots[j][...]
+
+
+def ride_shapes(n, items):
+    shapes, scratch = [], []
+    for kind, array in items:
+        inner = array.shape if kind == "gather1" else array.shape[1:]
+        if kind == "reduce":
+            shapes.append(jax.ShapeDtypeStruct(inner, F32))
+            scratch.append(pltpu.VMEM((n - 1,) + inner, array.dtype))
+        else:
+            out = (inner[0], n) + inner[1:]
+            shapes.append(jax.ShapeDtypeStruct(out, array.dtype))
+            scratch.append(pltpu.VMEM(out, array.dtype))
+    k = len(items)
+    sems = [pltpu.SemaphoreType.DMA((k, n - 1))] * 2 + [pltpu.SemaphoreType.DMA((k,))]
+    specs = [pl.BlockSpec(a.shape, functools.partial(origin, a.ndim)) for _, a in items]
+    outs = [pl.BlockSpec(a.shape, functools.partial(origin, len(a.shape))) for a in shapes]
+    return shapes, scratch + sems, specs, outs
+
+
+def origin(rank, i):
+    return (0,) * rank
+
+
 def tile_valid(info_ref, tile, step):
     row = lax.broadcasted_iota(jnp.int32, (tile, 1), 0)
     return info_ref[0] + step * tile + row < info_ref[1]
@@ -169,8 +250,18 @@
     return jnp.concatenate([past, cur_ref[...]], axis=1)
 
 
-def forward_kernel(info_ref, in_ref, past_ref, cur_ref, w_ref, t_ref, s_ref, hs_ref, ss_ref):
+def forward_kernel(
+    steps, axis, kinds, info_ref, in_ref, past_ref, cur_ref, w_ref, *refs
+):
+    k = len(kinds)
+    ins, (t_ref, s_ref, hs_ref, ss_ref) = refs[:k], refs[k : k + 4]
+    outs, slots, sems = refs[k + 4 : 2 * k + 4], refs[2 * k + 4 : 3 * k + 4], refs[3 * k + 4 :]
     i = pl.program_id(0)
+
+    @pl.when(i == 0)
+    def _():
+        ride_start(axis, kinds, ins, slots, *sems)
+
     tile, chans = cur_ref.shape
     joined = joined_tile(i == 0, in_ref, past_ref, cur_ref)
     mixed = jnp.dot(joined, w_ref[...], preferred_element_type=F32)
@@ -186,12 +277,25 @@
         hs_ref[0, j : j + 1, :] = jnp.sum(hidden[rows], axis=0, keepdims=True)
         ss_ref[0, j : j + 1, :] = jnp.sum(kept[rows], axis=0, keepdims=True)
 
+    @pl.when(i == steps - 1)
+    def _():
+        ride_finish(axis, kinds, ins, outs, slots, *sems)
+
 
 def backward_kernel(
-    steps, info_ref, in_ref, past_ref, cur_ref, t_ref, s_ref, dh_ref, dr_ref, w_ref,
-    sig_ref, first_ref, g_ref, acc_ref, later_ref,
+    steps, axis, kinds, info_ref, in_ref, past_ref, cur_ref, t_ref, s_ref, dh_ref, dr_ref, w_ref,
+    *refs,
 ):
+    k = len(kinds)
+    ins, (sig_ref, first_ref, g_ref) = refs[:k], refs[k : k + 3]
+    outs, (acc_ref, later_ref) = refs[k + 3 : 2 * k + 3], refs[2 * k + 3 : 2 * k + 5]
+    slots, sems = refs[2 * k + 5 : 3 * k + 5], refs[3 * k + 5 :]
     i = pl.program_id(0)
+
+    @pl.when(i == 0)
+    def _():
+        ride_start(axis, kinds, ins, slots, *sems)
+
     step = steps - 1 - i
     tile, chans = cur_ref.shape
 
@@ -228,6 +332,7 @@
     def _():
         first_ref[...] = d_joined[:, :chans].astype(BF16)
         g_ref[...] = acc_ref[...].astype(BF16)
+        ride_finish(axis, kinds, ins, outs, slots, *sems)
 
 
 def add_kernel(sig_ref, extra_ref, out_ref):
@@ -249,7 +354,9 @@
     )(d_sig, arriving)
 
 
-def conv_forward(info, incoming, signal, w_conv):
+def conv_forward(info, incoming, signal, w_conv, axis, collective, items):
+    kinds = tuple(kind for kind, _ in items)
+    shapes, scratch, specs, out_specs = ride_shapes(lax.axis_size(axis), items)
     samples, chans = signal.shape
     tile = DILATION_STEP
     steps, pools = samples // tile, tile // POOL
@@ -258,22 +365,29 @@
     gate = jax.ShapeDtypeStruct((samples, chans), F32)
     pooled = jax.ShapeDtypeStruct((steps, pools, chans), F32)
     return pl.pallas_call(
-        forward_kernel,
+        functools.partial(forward_kernel, steps, axis, kinds),
         grid=(steps,),
-        out_shape=(gate, gate, pooled, pooled),
+        out_shape=[gate, gate, pooled, pooled] + shapes,
         in_specs=[
             pl.BlockSpec(memory_space=pltpu.SMEM),
             pl.BlockSpec((tile, chans), lambda i: (0, 0)),
             pl.BlockSpec((tile, chans), lambda i: (jnp.maximum(i - 1, 0), 0)),
             block,
             pl.BlockSpec(w_conv.shape, lambda i: (0, 0)),
-        ],
-        out_specs=(block, block, sums, sums),
+        ]
+        + specs,
+        out_specs=[block, block, sums, sums] + out_specs,
+        scratch_shapes=scratch,
+        compiler_params=pltpu.CompilerParams(collective_id=collective, has_side_effects=True),
         name="conv_forward",
-    )(info, incoming, signal, signal, w_conv)
-
-
-def conv_backward(info, incoming, signal, t, s, d_hidden, d_resid, w_conv):
+    )(info, incoming, signal, signal, w_conv, *[array for _, array in items])
+
+
+def conv_backward(
+    info, incoming, signal, t, s, d_hidden, d_resid, w_conv, axis, collective, items
+):
+    kinds = tuple(kind for kind, _ in items)
+    shapes, scratch, specs, out_specs = ride_shapes(lax.axis_size(axis), items)
     samples, chans = signal.shape
     tile = DILATION_STEP
     steps, pools = samples // tile, tile // POOL
@@ -282,13 +396,14 @@
     sums = pl.BlockSpec((1, pools, chans), lambda i: (steps - 1 - i, 0, 0))
     whole = pl.BlockSpec(w_conv.shape, lambda i: (0, 0))
     return pl.pallas_call(
-        functools.partial(backward_kernel, steps),
+        functools.partial(backward_kernel, steps, axis, kinds),
         grid=(steps,),
-        out_shape=(
+        out_shape=[
             jax.ShapeDtypeStruct((samples, chans), BF16),
             jax.ShapeDtypeStruct((tile, chans), BF16),
             jax.ShapeDtypeStruct(w_conv.shape, BF16),
-        ),
+        ]
+        + shapes,
         in_specs=[
             pl.BlockSpec(memory_space=pltpu.SMEM),
             fixed,
@@ -299,11 +414,13 @@
             sums,
             sums,
             whole,
-        ],
-        out_specs=(block, fixed, whole),
-        scratch_shapes=[pltpu.VMEM(w_conv.shape, F32), pltpu.VMEM((tile, chans), BF16)],
+        ]
+        + specs,
+        out_specs=[block, fixed, whole] + out_specs,
+        scratch_shapes=[pltpu.VMEM(w_conv.shape, F32), pltpu.VMEM((tile, chans), BF16)] + scratch,
+        compiler_params=pltpu.CompilerParams(collective_id=collective, has_side_effects=True),
         name="conv_backward",
-    )(info, incoming, signal, signal, t, s, d_hidden, d_resid, w_conv)
+    )(info, incoming, signal, signal, t, s, d_hidden, d_resid, w_conv, *[a for _, a in items])
 
 
 def shifted(value, axis, by):
@@ -325,24 +442,22 @@
     flat = signal.reshape(samples, chans)
     incoming = shifted(flat[samples - DILATION_STEP :], "tm", 1)
     info = jnp.stack([tm * samples, lengths[0]]).astype(jnp.int32)
-    tanh_f, sig_g, h_sum, s_sum = conv_forward(info, incoming, flat, w_conv)
-    h_sum = h_sum.reshape(toks, chans)
-    h_part = jnp.dot(h_sum, w_res.astype(F32), precision=HIGH)
-    pooled = ((s_sum.reshape(toks, chans) + h_part) / POOL).astype(BF16)[None]
-    own_tok = dot("btc,cd->btd", pooled, w_in).astype(BF16)
     lens8 = jnp.broadcast_to(lengths.reshape(stays, 1, 1), (stays, 8, 128))
-    g_pool, g_dout, g_len = exchange(
-        "stream", 0, [("gather", pooled), ("gather", d_out), ("gather", lens8)]
-    )
-    group_pool = g_pool.reshape(group, toks, chans)
+    g_dout, g_len = exchange("stream", 0, [("gather", d_out), ("gather", lens8)])
     group_grad = g_dout.reshape(group, toks, width)
     group_len = g_len.reshape(group, 8, 128)[:, 0, 0]
     d_ctx = dot("btd,ed->bte", group_grad, w_out).astype(BF16)
     columns = width // tms
     grad_cols = group_grad.reshape(group, toks, tms, columns).transpose(2, 0, 1, 3)
-    all_pool, all_ctx, all_cols = exchange(
-        "tm", 1, [("gather1", group_pool), ("gather1", d_ctx), ("scatter1", grad_cols)]
-    )
+    tanh_f, sig_g, h_sum, s_sum, all_ctx, all_cols = conv_forward(
+        info, incoming, flat, w_conv, "tm", 6, [("gather1", d_ctx), ("scatter1", grad_cols)]
+    )
+    h_sum = h_sum.reshape(toks, chans)
+    h_part = jnp.dot(h_sum, w_res.astype(F32), precision=HIGH)
+    pooled = ((s_sum.reshape(toks, chans) + h_part) / POOL).astype(BF16)[None]
+    own_tok = dot("btc,cd->btd", pooled, w_in).astype(BF16)
+    (stay_pool,) = exchange("tm", 1, [("gather1", pooled)])
+    (all_pool,) = exchange("stream", 7, [("gather", stay_pool.reshape(stays, total, chans))])
     all_pool = all_pool.reshape(group, total, chans)
     all_ctx = all_ctx.reshape(group, total, heads * size)
     all_cols = all_cols.reshape(group, total, columns)
@@ -365,16 +480,9 @@
     g_in_cols = dot("btc,btd->cd", all_pool, all_cols)
     stream = lax.axis_index("stream")
     g_in_cols = lax.dynamic_slice_in_dim(g_in_cols, stream * in_rows, in_rows, 0)
-    s_out, s_group, s_in = exchange(
-        "stream",
-        2,
-        [
-            ("reduce", out_part.reshape(parts, stays, toks, width)),
-            ("reduce", own_group.reshape(parts, stays, toks, width)),
-            ("reduce", g_in_part.reshape(parts, in_rows, width)),
-        ],
-    )
-    out = (own_tok.astype(F32) + s_out).astype(BF16)
+    (s_group,) = exchange(
+        "stream", 2, [("reduce", own_group.reshape(parts, stays, toks, width))]
+    )
     d_tok = (s_group + d_out.astype(F32)).astype(BF16)
     d_pooled = dot("btd,cd->btc", d_tok, w_in)
     d_res16 = (d_pooled / POOL).astype(BF16).reshape(toks, chans)
@@ -383,7 +491,7 @@
         d_res16, w_res, (((1,), (1,)), ((), ())), preferred_element_type=F32
     )
     per_tile = (samples // DILATION_STEP, DILATION_STEP // POOL, chans)
-    d_sig, first, g_conv = conv_backward(
+    d_sig, first, g_conv, s_out, s_in = conv_backward(
         info,
         incoming,
         flat,
@@ -392,7 +500,14 @@
         d_hidden.reshape(per_tile),
         d_res16.astype(F32).reshape(per_tile),
         w_conv,
-    )
+        "stream",
+        8,
+        [
+            ("reduce", out_part.reshape(parts, stays, toks, width)),
+            ("reduce", g_in_part.reshape(parts, in_rows, width)),
+        ],
+    )
+    out = (own_tok.astype(F32) + s_out).astype(BF16)
     arriving = shifted(first, "tm", -1)
     d_signal = add_last(d_sig, arriving)[None]
     s_conv, s_res = exchange(
@@ -415,9 +530,9 @@
         "tm",
         5,
         [
-            ("gather", t_conv),
-            ("gather", t_res),
-            ("gather", g_in_cols.astype(BF16)),
+            ("gatherf", t_conv),
+            ("gatherf", t_res),
+            ("gatherf", g_in_cols.astype(BF16)),
         ],
     )
     sum_conv = a_conv.reshape(2 * chans // parts, 2 * chans).astype(F32)

time: 186 us -> 172 us (0.925)
  Pallas kernels: 130 us -> 119 us
  waiting for transfers between devices: 8.02 us -> 0.01 us
  local copies, waits for them, and re-layouts: 10.5 us -> 16.4 us
  other arithmetic: 8.36 us -> 5.41 us
  matrix products: 19.5 us -> 22.2 us
    pallas_call x6 -> x7, Pallas kernels: 85.8 us -> 65.6 us  [exchange(): pl.pallas_call(functools.partial(exchange_kernel, axis, n, kinds), out_sh...]
    pallas_call x2, Pallas kernels: 29.8 us -> 38.7 us  [the longest x1 20 us: conv_forward(): pl.pallas_call(functools.partial(forward_kernel, steps, axis, kinds), gri...]
    ppermute x2, waiting for transfers between devices: 8.02 us -> 0.01 us  [shifted(): return lax.ppermute(value, axis, pairs)]
    unnamed x37 -> x40, local copies, waits for them, and re-layouts: 3.21 us -> 8.36 us
    convert_element_type x2 -> x0, other arithmetic: 3.02 us -> none  [the longest x1 1.63 us: local(): sum_conv = a_conv.reshape(2 * chans // parts, 2 * chans).astype(F32)]
    dot_general x11, matrix products: 18.2 us -> 20.9 us  [dot(): return jnp.einsum(eq, a, b, preferred_element_type=F32)]
  transfers between devices with their start and end apart: 2 -> 2, of which waited for: 2 -> 0; matrix products, arithmetic and copies ran while one was open for 2% -> 6% of each run, Pallas kernels for 0% -> 25%
where the time goes in v3:
time: 172 us; the launch traced here: 170 us
  Pallas kernels  119 us (69%)
  matrix products  22.2 us (13%)
  local copies, waits for them, and re-layouts  16.4 us (10%)
  starting transfers between devices  6.2 us (4%)
  other arithmetic  5.41 us (3%)
    pallas_call x7, Pallas kernels, exchange(): pl.pallas_call(functools.partial(exchange_kernel, axis, n, kinds), out_sh...  65.6 us
    dot_general x11, matrix products, dot(): return jnp.einsum(eq, a, b, preferred_element_type=F32)  20.9 us
    pallas_call x1, Pallas kernels, conv_forward(): pl.pallas_call(functools.partial(forward_kernel, steps, axis, kinds), gri...  20 us
    pallas_call x1, Pallas kernels, conv_backward(): pl.pallas_call(functools.partial(backward_kernel, steps, axis, kinds), gr...  18.7 us
    pallas_call x1, Pallas kernels, attention(): pl.pallas_call(functools.partial(attention_kernel, heads, size, 1.0 / mat...  12.6 us
    unnamed x40, local copies, waits for them, and re-layouts  8.36 us
    ppermute x2, starting transfers between devices, shifted(): return lax.ppermute(value, axis, pairs)  6.2 us
  transfers between devices with their start and end apart: 2, of which 0 were waited for; matrix products, arithmetic and copies ran while one was open for 6% of the time, Pallas kernels for 25%

profile of v3, /device:TPU:0, one launch (start us, length us, event | category | flops | bytes accessed | tf_op | source)
XLA Modules:
  0.0 170.4 jit_solution(10719402927848390502)
XLA Ops:
  0.6 1.1 slice_bitcast_fusion
  1.7 4.9 %collective-permute-start = (bf16[512,256]{1,0:T(8,128)(2,1)S(1)}, bf16[512,256]{1,0:T(8,128)(2,1)S(1)}, u32[]{:S(2)}, u32[]{:S(2)}) collective-permute-start(bf16[512,256]{1,0:T(8,128)(2,1)S(1)} %slice_bitcast_fusion), channel_id=1, source_target_pairs={{0,4},{4,8},{8,12},{12,16},{16,20},{20,24},{24,28},{1,5},{5,9},{9,... | collective-permute-start | bytes 786440 | tf_op jit(solution)/shard_map/ppermute | solution.py:429
  7.9 6.8 %exchange_stream_0.1 = (bf16[4,1,24,1024]{3,2,1,0:T(8,128)(2,1)}, s32[4,1,8,128]{3,2,1,0:T(8,128)}) custom-call(bf16[1,24,1024]{2,1,0:T(8,128)(2,1)} %refs_0_.1, s32[1,8,128]{2,1,0:T(8,128)} %broadcast_in_dim.16.refs_1_), custom_call_target="tpu_custom_call" | custom-call | tf_op jit(solution)/shard_map/exchange_stream_0/pallas_call | solution.py:102
  14.7 1.4 slice_reduce_fusion.len_ref
  16.8 1.0 copy.23
  18.5 2.1 %convolution_convert_fusion.3.refs_0_ = bf16[4,24,256]{2,1,0:T(8,128)(2,1)} fusion(bf16[256,1024]{1,0:T(8,128)(2,1)} %param.14, bf16[4,1,24,1024]{3,2,1,0:T(8,128)(2,1)} %get-tuple-element.29), kind=kOutput, calls=%fused_computation.26 | convolution fusion | flops 50356224 | bytes 770048 | tf_op jit(solution)/shard_map/btd,ed->bte/dot_general | solution.py:23
  21.2 20.0 %conv_forward.1 = (f32[6144,256]{1,0:T(8,128)}, f32[6144,256]{1,0:T(8,128)}, f32[12,2,256]{2,1,0:T(2,128)}, f32[12,2,256]{2,1,0:T(2,128)}, bf16[4,8,24,256]{3,2,...) custom-call(s32[2]{0:T(128)} %pad_add_fusion.info_ref, bf16[512,256]{1,0:T(8,128)(2,1)} %copy-done.8, ...), custom_call_target="tpu_custom_call" | custom-call | tf_op jit(solution)/shard_map/conv_forward/pallas_call | solution.py:367
  43.6 8.7 %exchange_tm_1.1 = bf16[1,8,24,256]{3,2,1,0:T(8,128)(2,1)} custom-call(bf16[1,24,256]{2,1,0:T(8,128)(2,1)} %bitcast.118), custom_call_target="tpu_custom_call" | custom-call | tf_op jit(solution)/shard_map/exchange_tm_1/pallas_call | solution.py:102
  52.3 7.9 %exchange_stream_7.1 = bf16[4,1,192,256]{3,2,1,0:T(8,128)(2,1)} custom-call(bf16[1,192,256]{2,1,0:T(8,128)(2,1)} %bitcast.115), custom_call_target="tpu_custom_call" | custom-call | tf_op jit(solution)/shard_map/exchange_stream_7/pallas_call | solution.py:102
  60.3 2.0 %convolution_bitcast_fusion.3 = bf16[256,128]{1,0:T(8,128)(2,1)} fusion(bf16[4,192,128]{2,1,0:T(8,128)(2,1)} %bitcast.108, bf16[4,1,192,256]{3,2,1,0:T(8,128)(2,1)} %exchange_stream_7.1), kind=kOutput, calls=%fused_computation.25 | convolution fusion | flops 50331648 | bytes 655360 | tf_op jit(solution)/shard_map/btc,btd->cd/dot_general | solution.py:23
  62.3 1.7 fusion.1
  65.1 2.4 %fusion.12.proj_ref = bf16[4,192,768]{2,1,0:T(8,128)(2,1)} fusion(bf16[4,192,1024]{2,1,0:T(8,128)(2,1)S(1)} %fusion.2, bf16[1024,768]{1,0:T(8,128)(2,1)S(1)} %copy-done), kind=kOutput, calls=%fused_computation.17 | convolution fusion | flops 1208549376 | bytes 4325376 | tf_op jit(solution)/shard_map/btd,de->bte/dot_general | solution.py:23
  67.5 12.6 %attention.1 = (bf16[4,192,256]{2,1,0:T(8,128)(2,1)}, bf16[4,192,768]{2,1,0:T(8,128)(2,1)}) custom-call(s32[4]{0:T(128)} %slice_reduce_fusion.len_ref, bf16[4,192,768]{2,1,0:T(8,128)(2,1)} %fusion.12.proj_ref, bf16[4,192,256]{2,1,0:T(8,128)(2,1)} %bitcast.114), custom_call_target="tpu_custom_call" | custom-call | tf_op jit(solution)/shard_map/attention/pallas_call | solution.py:157
  80.1 2.0 %convolution_bitcast_fusion.2 = f32[256,128]{1,0:T(8,128)} fusion(bf16[4,192,256]{2,1,0:T(8,128)(2,1)} %get-tuple-element.37, bf16[4,192,128]{2,1,0:T(8,128)(2,1)S(1)} %bitcast.109), kind=kOutput, calls=%fused_computation.24 | convolution fusion | flops 50331648 | bytes 720896 | tf_op jit(solution)/shard_map/bte,btd->ed/dot_general | solution.py:23
  82.0 1.7 fusion.16.refs_0_
  83.7 2.8 %fusion.8 = f32[4,192,1024]{2,1,0:T(8,128)S(1)} fusion(bf16[4,192,768]{2,1,0:T(8,128)(2,1)} %get-tuple-element.36, bf16[1024,768]{1,0:T(8,128)(2,1)S(1)} %copy-done), kind=kOutput, calls=%fused_computation.13 | convolution fusion | flops 1207959552 | bytes 5898240 | tf_op jit(solution)/shard_map/bte,de->btd/dot_general | solution.py:23
  86.6 1.5 fusion.6
  88.1 1.4 fusion.15
  90.2 6.6 %exchange_stream_2.1 = f32[1,24,1024]{2,1,0:T(8,128)} custom-call(bf16[4,1,24,1024]{3,2,1,0:T(8,128)(2,1)} %dynamic-slice_bitcast_fusion.refs_0_), custom_call_target="tpu_custom_call" | custom-call | tf_op jit(solution)/shard_map/exchange_stream_2/pallas_call | solution.py:102
  96.9 1.1 fusion.19
  98.8 1.0 convolution_convert_fusion.2
  99.8 2.0 %convolution_bitcast_fusion.1 = f32[128,768]{1,0:T(8,128)} fusion(bf16[4,192,768]{2,1,0:T(8,128)(2,1)S(1)} %copy-done.7, bf16[4,192,1024]{2,1,0:T(8,128)(2,1)} %copy-done.3, s32[]{:T(128)S(6)} %select_n.12), kind=kOutput, calls=%fused_computation.20 | convolution fusion | flops 150994944 | bytes 1769476 | tf_op jit(solution)/shard_map/btd,bte->de/dot_general | solution.py:23
  102.5 18.7 %conv_backward.1 = (bf16[6144,256]{1,0:T(8,128)(2,1)}, bf16[512,256]{1,0:T(8,128)(2,1)}, bf16[512,512]{1,0:T(8,128)(2,1)}, f32[1,24,1024]{2,1,0:T(8,128)}, f32[64,1024]{1,0:T(8,128)}) custom-call(s32[2]{0:T(128)} %pad_add_fusion.info_ref, bf16[512,256]{1,0:T(8,128)(2,1)} %copy-done.8, bf16[6144,256]{1,0:T(8,128)(2,1)} %bitcast.103, ...), custom_call_target="tpu_custom_call" | custom-call | tf_op jit(solution)/shard_map/conv_backward/pallas_call | solution.py:398
  121.2 1.7 %add_convert_fusion = bf16[1,24,1024]{2,1,0:T(8,128)(2,1)} fusion(f32[1,24,1024]{2,1,0:T(8,128)} %get-tuple-element.38, bf16[24,256]{1,0:T(8,128)(2,1)S(1)} %copy-done.16, bf16[256,1024]{1,0:T(8,128)(2,1)S(1)} %copy-done.2), kind=kOutput, calls=%fused_computation.46 | convolution fusion | flops 12681216 | bytes 684032 | tf_op jit(solution)/shard_map/btc,cd->btd/dot_general | solution.py:23
  122.9 1.3 collective-permute-start.1
  124.2 1.3 dynamic-slice_convert_fusion.refs_2_
  125.6 11.6 %exchange_stream_3.1 = (bf16[128,512]{1,0:T(8,128)(2,1)}, bf16[64,256]{1,0:T(8,128)(2,1)}) custom-call(bf16[4,128,512]{2,1,0:T(8,128)(2,1)} %bitcast.112, bf16[4,64,256]{2,1,0:T(8,128)(2,1)} %bitcast.113), custom_call_target="tpu_custom_call" | custom-call | tf_op jit(solution)/shard_map/exchange_stream_3/pallas_call | solution.py:102
  137.1 12.0 %exchange_tm_4.1 = (bf16[16,512]{1,0:T(8,128)(2,1)}, bf16[8,256]{1,0:T(8,128)(2,1)}) custom-call(bf16[8,16,512]{2,1,0:T(8,128)(2,1)} %bitcast.117, bf16[8,8,256]{2,1,0:T(8,128)(2,1)} %bitcast.120), custom_call_target="tpu_custom_call" | custom-call | tf_op jit(solution)/shard_map/exchange_tm_4/pallas_call | solution.py:102
  149.1 11.9 %exchange_tm_5.1 = (f32[8,16,512]{2,1,0:T(8,128)}, f32[8,8,256]{2,1,0:T(8,128)}, f32[8,64,128]{2,1,0:T(8,128)}) custom-call(bf16[16,512]{1,0:T(8,128)(2,1)} %get-tuple-element.44.refs_0_, bf16[8,256]{1,0:T(8,128)(2,1)} %get-tuple-element.45.refs_1_, bf16[64,128]{1,0:T(8,128)(2,1)} %dynamic-slice_convert_fusion.refs_2_), custom_call_target="tpu_custom_call" | custom-call | tf_op jit(solution)/shard_map/exchange_tm_5/pallas_call | solution.py:102
  161.1 1.7 bitcast_add_fusion
  163.5 1.8 %add_last.1 = bf16[6144,256]{1,0:T(8,128)(2,1)} custom-call(bf16[6144,256]{1,0:T(8,128)(2,1)} %get-tuple-element.39.sig_ref, bf16[512,256]{1,0:T(8,128)(2,1)} %copy-done.13), custom_call_target="tpu_custom_call", output_to_operand_aliasing={{}: (0, {})} | custom-call | tf_op jit(solution)/shard_map/add_last/pallas_call | solution.py:346
  165.2 3.8 %copy.34 = bf16[1,6144,256]{2,1,0:T(8,128)(2,1)} copy(bf16[1,6144,256]{2,1,0:T(8,128)(2,1)} %bitcast.105) | data formatting | bytes 6291456
  (54 shorter events, 10.4 us)
Async XLA Ops:
  0.6 64.5 %copy-start = (bf16[1024,768]{1,0:T(8,128)(2,1)S(1)}, bf16[1024,768]{1,0:T(8,128)(2,1)}, u32[]{:S(2)}) copy-start(bf16[1024,768]{1,0:T(8,128)(2,1)} %param.13) | copy-start | bytes 4718596
  1.7 18.8 %collective-permute-start = (bf16[512,256]{1,0:T(8,128)(2,1)S(1)}, bf16[512,256]{1,0:T(8,128)(2,1)S(1)}, u32[]{:S(2)}, u32[]{:S(2)}) collective-permute-start(bf16[512,256]{1,0:T(8,128)(2,1)S(1)} %slice_bitcast_fusion), channel_id=1, source_target_pairs={{0,4},{4,8},{8,12},{12,16},{16,20},{20,24},{24,28},{1,5},{5,9},{9,... | collective-permute-start | bytes 786440 | tf_op jit(solution)/shard_map/ppermute | solution.py:429
  20.5 0.7 copy-start.8
  21.2 21.6 %copy-start.10 = (bf16[256,256]{1,0:T(8,128)(2,1)S(1)}, bf16[256,256]{1,0:T(8,128)(2,1)}, u32[]{:S(2)}) copy-start(bf16[256,256]{1,0:T(8,128)(2,1)} %param.11) | copy-start | bytes 393220
  41.2 21.1 %copy-start.2 = (bf16[256,1024]{1,0:T(8,128)(2,1)S(1)}, bf16[256,1024]{1,0:T(8,128)(2,1)}, u32[]{:S(2)}) copy-start(bf16[256,1024]{1,0:T(8,128)(2,1)} %param.12) | copy-start | bytes 1572868
  63.9 1.1 copy-start.4
  65.1 2.4 %copy-start.3 = (bf16[4,192,1024]{2,1,0:T(8,128)(2,1)}, bf16[4,192,1024]{2,1,0:T(8,128)(2,1)S(1)}, u32[]{:S(2)}) copy-start(bf16[4,192,1024]{2,1,0:T(8,128)(2,1)S(1)} %fusion.2) | copy-start | bytes 4718596
  67.5 12.6 %copy-start.9 = (bf16[4,8,24,128]{3,2,1,0:T(8,128)(2,1)S(1)}, bf16[4,8,24,128]{3,2,1,0:T(8,128)(2,1)}, u32[]{:S(2)}) copy-start(bf16[4,8,24,128]{3,2,1,0:T(8,128)(2,1)} %get-tuple-element.46) | copy-start | bytes 589828
  67.5 14.5 %copy-start.1 = (bf16[256,1024]{1,0:T(8,128)(2,1)S(1)}, bf16[256,1024]{1,0:T(8,128)(2,1)}, u32[]{:S(2)}) copy-start(bf16[256,1024]{1,0:T(8,128)(2,1)} %param.14) | copy-start | bytes 1572868
  83.7 2.8 %copy-start.5 = (bf16[4,192,1024]{2,1,0:T(8,128)(2,1)S(1)}, bf16[4,192,1024]{2,1,0:T(8,128)(2,1)}, u32[]{:S(2)}) copy-start(bf16[4,192,1024]{2,1,0:T(8,128)(2,1)} %copy-done.4) | copy-start | bytes 4718596
  86.5 1.5 copy-start.6
  88.1 8.8 %copy-start.15 = (bf16[1,24,1024]{2,1,0:T(8,128)(2,1)S(1)}, bf16[1,24,1024]{2,1,0:T(8,128)(2,1)}, u32[]{:S(2)}) copy-start(bf16[1,24,1024]{2,1,0:T(8,128)(2,1)} %refs_0_.1) | copy-start | bytes 147460
  88.1 10.6 %copy-start.11 = (bf16[256,256]{1,0:T(8,128)(2,1)S(1)}, bf16[256,256]{1,0:T(8,128)(2,1)}, u32[]{:S(2)}) copy-start(bf16[256,256]{1,0:T(8,128)(2,1)} %param.11) | copy-start | bytes 393220
  89.5 10.3 %copy-start.7 = (bf16[4,192,768]{2,1,0:T(8,128)(2,1)S(1)}, bf16[4,192,768]{2,1,0:T(8,128)(2,1)}, u32[]{:S(2)}) copy-start(bf16[4,192,768]{2,1,0:T(8,128)(2,1)} %get-tuple-element.36) | copy-start | bytes 3538948
  102.5 18.7 %copy-start.16 = (bf16[24,256]{1,0:T(8,128)(2,1)S(1)}, bf16[24,256]{1,0:T(8,128)(2,1)}, u32[]{:S(2)}) copy-start(bf16[24,256]{1,0:T(8,128)(2,1)} %multiply_convert_fusion) | copy-start | bytes 36868
  121.2 39.9 %copy-start.12 = (f32[64,1024]{1,0:T(8,128)S(1)}, f32[64,1024]{1,0:T(8,128)}, u32[]{:S(2)}) copy-start(f32[64,1024]{1,0:T(8,128)} %get-tuple-element.49) | copy-start | bytes 786436
  122.9 39.8 %collective-permute-start.1 = (bf16[512,256]{1,0:T(8,128)(2,1)}, bf16[512,256]{1,0:T(8,128)(2,1)S(1)}, u32[]{:S(2)}, u32[]{:S(2)}) collective-permute-start(bf16[512,256]{1,0:T(8,128)(2,1)} %get-tuple-element.40), channel_id=1, source_target_pairs={{4,0},{8,4},{12,8},{16,12},{20,16},{24,20},{28,24},{5,1},{9,5},{13... | collective-permute-start | bytes 786440 | tf_op jit(solution)/shard_map/ppermute | solution.py:429
  162.8 0.7 copy-start.13
  165.2 3.8 %copy-start.14 = (f32[8,16,512]{2,1,0:T(8,128)S(1)}, f32[8,16,512]{2,1,0:T(8,128)}, u32[]{:S(2)}) copy-start(f32[8,16,512]{2,1,0:T(8,128)} %get-tuple-element.47) | copy-start | bytes 786436
  165.2 4.5 %copy-start.17 = (f32[8,8,256]{2,1,0:T(8,128)S(1)}, f32[8,8,256]{2,1,0:T(8,128)}, u32[]{:S(2)}) copy-start(f32[8,8,256]{2,1,0:T(8,128)} %get-tuple-element.48) | copy-start | bytes 196612

commit v4 on v3

--- a/solution.py
+++ b/solution.py
@@ -335,23 +335,70 @@
         ride_finish(axis, kinds, ins, outs, slots, *sems)
 
 
-def add_kernel(sig_ref, extra_ref, out_ref):
-    out_ref[...] = (sig_ref[...].astype(F32) + extra_ref[...].astype(F32)).astype(BF16)
-
-
-def add_last(d_sig, arriving):
-    samples, chans = d_sig.shape
-    rows = arriving.shape[0]
-    last = pl.BlockSpec((rows, chans), lambda i: (samples // rows - 1, 0))
+def final_kernel(axis, n, *refs):
+    ins, outs, slots, mine, lands = refs[:3], refs[3:6], refs[6:8], refs[8:10], refs[10:13]
+    send, recv, keep = refs[13:]
+    me = lax.axis_index(axis)
+    barrier = pltpu.get_barrier_semaphore()
+    for d in range(1, n):
+        pl.semaphore_signal(
+            barrier, inc=1, device_id={axis: lax.rem(me + d, n)}, device_id_type=MESH
+        )
+    pl.semaphore_wait(barrier, n - 1)
+
+    def push(row, d, src, dst):
+        copy = pltpu.make_async_remote_copy(
+            src_ref=src,
+            dst_ref=dst,
+            send_sem=send.at[row, d - 1],
+            recv_sem=recv.at[row, d - 1],
+            device_id={axis: lax.rem(me + d, n)},
+            device_id_type=MESH,
+        )
+        copy.start()
+        return copy
+
+    parts = [
+        push(j, d, ins[j].at[lax.rem(me + d, n)], slots[j].at[d - 1])
+        for j in range(2)
+        for d in range(1, n)
+    ]
+    rest = [push(2, d, ins[2], lands[2].at[me]) for d in range(1, n)]
+    for copy in parts:
+        copy.wait()
+    for j in range(2):
+        total = ins[j][me].astype(F32)
+        for d in range(1, n):
+            total += slots[j][d - 1].astype(F32)
+        mine[j][...] = total.astype(BF16)
+    for j, src in enumerate((mine[0], mine[1], ins[2])):
+        copy = pltpu.make_async_copy(src, lands[j].at[me], keep.at[j])
+        copy.start()
+        rest.append(copy)
+    rest += [push(3 + j, d, mine[j], lands[j].at[me]) for j in range(2) for d in range(1, n)]
+    for copy in rest:
+        copy.wait()
+    for j in range(3):
+        outs[j][...] = lands[j][...].astype(F32)
+
+
+def final_sums(axis, collective, conv, res, cols):
+    n = lax.axis_size(axis)
+    shapes = [conv.shape, res.shape, (n,) + cols.shape]
+    sums = [conv.shape[1:], res.shape[1:]]
     return pl.pallas_call(
-        add_kernel,
-        grid=(1,),
-        out_shape=jax.ShapeDtypeStruct(d_sig.shape, BF16),
-        in_specs=[last, pl.BlockSpec((rows, chans), lambda i: (0, 0))],
-        out_specs=last,
-        input_output_aliases={0: 0},
-        name="add_last",
-    )(d_sig, arriving)
+        functools.partial(final_kernel, axis, n),
+        out_shape=[jax.ShapeDtypeStruct(a, F32) for a in shapes],
+        in_specs=[VMEM_SPEC] * 3,
+        out_specs=[VMEM_SPEC] * 3,
+        scratch_shapes=[pltpu.VMEM((n - 1,) + a, BF16) for a in sums]
+        + [pltpu.VMEM(a, BF16) for a in sums]
+        + [pltpu.VMEM(a, BF16) for a in shapes]
+        + [pltpu.SemaphoreType.DMA((5, n - 1))] * 2
+        + [pltpu.SemaphoreType.DMA((3,))],
+        compiler_params=pltpu.CompilerParams(collective_id=collective, has_side_effects=True),
+        name="final_sums",
+    )(conv, res, cols)
 
 
 def conv_forward(info, incoming, signal, w_conv, axis, collective, items):
@@ -509,7 +556,9 @@
     )
     out = (own_tok.astype(F32) + s_out).astype(BF16)
     arriving = shifted(first, "tm", -1)
-    d_signal = add_last(d_sig, arriving)[None]
+    edge = samples - DILATION_STEP
+    last = (d_sig[edge:].astype(F32) + arriving.astype(F32)).astype(BF16)
+    d_signal = jnp.concatenate([d_sig[:edge], last], axis=0)[None]
     s_conv, s_res = exchange(
         "stream",
         3,
@@ -518,22 +567,12 @@
             ("reduceb", g_res.astype(BF16).reshape(parts, -1, chans)),
         ],
     )
-    t_conv, t_res = exchange(
+    a_conv, a_res, a_in = final_sums(
         "tm",
         4,
-        [
-            ("reduceb", s_conv.reshape(tms, -1, 2 * chans)),
-            ("reduceb", s_res.reshape(tms, -1, chans)),
-        ],
-    )
-    a_conv, a_res, a_in = exchange(
-        "tm",
-        5,
-        [
-            ("gatherf", t_conv),
-            ("gatherf", t_res),
-            ("gatherf", g_in_cols.astype(BF16)),
-        ],
+        s_conv.reshape(tms, -1, 2 * chans),
+        s_res.reshape(tms, -1, chans),
+        g_in_cols.astype(BF16),
     )
     sum_conv = a_conv.reshape(2 * chans // parts, 2 * chans).astype(F32)
     sum_res = a_res.reshape(chans // parts, chans).astype(F32)

time: 172 us -> 169 us (0.983)
  Pallas kernels: 119 us -> 113 us
  other arithmetic: 5.41 us -> 10.1 us
    pallas_call x7 -> x5, Pallas kernels: 65.6 us -> 41.7 us  [exchange(): pl.pallas_call(functools.partial(exchange_kernel, axis, n, kinds), out_sh...]
    pallas_call x1, Pallas kernels: 1.79 us -> 20 us  [final_sums(): pl.pallas_call(functools.partial(final_kernel, axis, n), out_shape=[jax.S...]
    unnamed x40 -> x37, local copies, waits for them, and re-layouts: 8.36 us -> 3.06 us
    broadcast_in_dim x0 -> x1, other arithmetic: none -> 3.73 us  [local(): d_signal = jnp.concatenate([d_sig[:edge], last], axis=0)[None]]
    slice x0 -> x1, local copies, waits for them, and re-layouts: none -> 3.62 us  [local(): d_signal = jnp.concatenate([d_sig[:edge], last], axis=0)[None]]
  transfers between devices with their start and end apart: 2 -> 2, of which waited for: 0 -> 0; matrix products, arithmetic and copies ran while one was open for 6% -> 8% of each run, Pallas kernels for 25% -> 23%
where the time goes in v4:
time: 169 us; the launch traced here: 168 us
  Pallas kernels  113 us (67%)
  matrix products  22.2 us (13%)
  local copies, waits for them, and re-layouts  14.7 us (9%)
  other arithmetic  10.1 us (6%)
  starting transfers between devices  6.2 us (4%)
    pallas_call x5, Pallas kernels, exchange(): pl.pallas_call(functools.partial(exchange_kernel, axis, n, kinds), out_sh...  41.7 us
    dot_general x11, matrix products, dot(): return jnp.einsum(eq, a, b, preferred_element_type=F32)  20.9 us
    pallas_call x1, Pallas kernels, conv_forward(): pl.pallas_call(functools.partial(forward_kernel, steps, axis, kinds), gri...  20 us
    pallas_call x1, Pallas kernels, final_sums(): pl.pallas_call(functools.partial(final_kernel, axis, n), out_shape=[jax.S...  20 us
    pallas_call x1, Pallas kernels, conv_backward(): pl.pallas_call(functools.partial(backward_kernel, steps, axis, kinds), gr...  18.7 us
    pallas_call x1, Pallas kernels, attention(): pl.pallas_call(functools.partial(attention_kernel, heads, size, 1.0 / mat...  12.5 us
    ppermute x2, starting transfers between devices, shifted(): return lax.ppermute(value, axis, pairs)  6.2 us
    broadcast_in_dim x1, other arithmetic, local(): d_signal = jnp.concatenate([d_sig[:edge], last], axis=0)[None]  3.73 us
  transfers between devices with their start and end apart: 2, of which 0 were waited for; matrix products, arithmetic and copies ran while one was open for 8% of the time, Pallas kernels for 23%

profile of v4, /device:TPU:0, one launch (start us, length us, event | category | flops | bytes accessed | tf_op | source)
XLA Modules:
  0.0 167.7 jit_solution(13160960879089267762)
XLA Ops:
  0.6 1.1 slice_bitcast_fusion
  1.7 4.9 %collective-permute-start = (bf16[512,256]{1,0:T(8,128)(2,1)S(1)}, bf16[512,256]{1,0:T(8,128)(2,1)S(1)}, u32[]{:S(2)}, u32[]{:S(2)}) collective-permute-start(bf16[512,256]{1,0:T(8,128)(2,1)S(1)} %slice_bitcast_fusion), channel_id=1, source_target_pairs={{0,4},{4,8},{8,12},{12,16},{16,20},{20,24},{24,28},{1,5},{5,9},{9,... | collective-permute-start | bytes 786440 | tf_op jit(solution)/shard_map/ppermute | solution.py:476
  7.9 6.8 %exchange_stream_0.1 = (bf16[4,1,24,1024]{3,2,1,0:T(8,128)(2,1)}, s32[4,1,8,128]{3,2,1,0:T(8,128)}) custom-call(bf16[1,24,1024]{2,1,0:T(8,128)(2,1)} %refs_0_.1, s32[1,8,128]{2,1,0:T(8,128)} %broadcast_in_dim.16.refs_1_), custom_call_target="tpu_custom_call" | custom-call | tf_op jit(solution)/shard_map/exchange_stream_0/pallas_call | solution.py:102
  14.8 1.4 slice_reduce_fusion.len_ref
  16.7 1.0 copy.22
  18.4 2.1 %convolution_convert_fusion.3.refs_0_ = bf16[4,24,256]{2,1,0:T(8,128)(2,1)} fusion(bf16[256,1024]{1,0:T(8,128)(2,1)} %param.14, bf16[4,1,24,1024]{3,2,1,0:T(8,128)(2,1)} %get-tuple-element.27), kind=kOutput, calls=%fused_computation.27 | convolution fusion | flops 50356224 | bytes 770048 | tf_op jit(solution)/shard_map/btd,ed->bte/dot_general | solution.py:23
  21.2 20.0 %conv_forward.1 = (f32[6144,256]{1,0:T(8,128)}, f32[6144,256]{1,0:T(8,128)}, f32[12,2,256]{2,1,0:T(2,128)}, f32[12,2,256]{2,1,0:T(2,128)}, bf16[4,8,24,256]{3,2,...) custom-call(s32[2]{0:T(128)} %pad_add_fusion.info_ref, bf16[512,256]{1,0:T(8,128)(2,1)} %copy-done.8, ...), custom_call_target="tpu_custom_call" | custom-call | tf_op jit(solution)/shard_map/conv_forward/pallas_call | solution.py:414
  43.5 8.7 %exchange_tm_1.1 = bf16[1,8,24,256]{3,2,1,0:T(8,128)(2,1)} custom-call(bf16[1,24,256]{2,1,0:T(8,128)(2,1)} %bitcast.118), custom_call_target="tpu_custom_call" | custom-call | tf_op jit(solution)/shard_map/exchange_tm_1/pallas_call | solution.py:102
  52.3 7.9 %exchange_stream_7.1 = bf16[4,1,192,256]{3,2,1,0:T(8,128)(2,1)} custom-call(bf16[1,192,256]{2,1,0:T(8,128)(2,1)} %bitcast.115), custom_call_target="tpu_custom_call" | custom-call | tf_op jit(solution)/shard_map/exchange_stream_7/pallas_call | solution.py:102
  60.2 2.0 %convolution_bitcast_fusion.3 = bf16[256,128]{1,0:T(8,128)(2,1)} fusion(bf16[4,192,128]{2,1,0:T(8,128)(2,1)} %bitcast.108, bf16[4,1,192,256]{3,2,1,0:T(8,128)(2,1)} %exchange_stream_7.1), kind=kOutput, calls=%fused_computation.26 | convolution fusion | flops 50331648 | bytes 655360 | tf_op jit(solution)/shard_map/btc,btd->cd/dot_general | solution.py:23
  62.2 1.7 fusion.1
  64.3 2.4 %fusion.12.proj_ref = bf16[4,192,768]{2,1,0:T(8,128)(2,1)} fusion(bf16[4,192,1024]{2,1,0:T(8,128)(2,1)S(1)} %fusion.2, bf16[1024,768]{1,0:T(8,128)(2,1)S(1)} %copy-done), kind=kOutput, calls=%fused_computation.18 | convolution fusion | flops 1208549376 | bytes 4325376 | tf_op jit(solution)/shard_map/btd,de->bte/dot_general | solution.py:23
  66.7 12.5 %attention.1 = (bf16[4,192,256]{2,1,0:T(8,128)(2,1)}, bf16[4,192,768]{2,1,0:T(8,128)(2,1)}) custom-call(s32[4]{0:T(128)} %slice_reduce_fusion.len_ref, bf16[4,192,768]{2,1,0:T(8,128)(2,1)} %fusion.12.proj_ref, bf16[4,192,256]{2,1,0:T(8,128)(2,1)} %bitcast.114), custom_call_target="tpu_custom_call" | custom-call | tf_op jit(solution)/shard_map/attention/pallas_call | solution.py:157
  79.2 2.0 %convolution_bitcast_fusion.2 = f32[256,128]{1,0:T(8,128)} fusion(bf16[4,192,256]{2,1,0:T(8,128)(2,1)} %get-tuple-element.35, bf16[4,192,128]{2,1,0:T(8,128)(2,1)S(1)} %bitcast.109), kind=kOutput, calls=%fused_computation.25 | convolution fusion | flops 50331648 | bytes 720896 | tf_op jit(solution)/shard_map/bte,btd->ed/dot_general | solution.py:23
  81.2 1.7 %fusion.16.refs_0_ = bf16[4,1,24,1024]{3,2,1,0:T(8,128)(2,1)} fusion(bf16[256,1024]{1,0:T(8,128)(2,1)S(1)} %copy-done.1, bf16[4,192,256]{2,1,0:T(8,128)(2,1)} %get-tuple-element.35, s32[]{:T(128)S(6)} %select_n.10), kind=kOutput, calls=%fused_computation.23 | convolution fusion | flops 50429952 | bytes 770052 | tf_op jit(solution)/shard_map/bte,ed->btd/dot_general | solution.py:23
  82.9 2.8 %fusion.8 = f32[4,192,1024]{2,1,0:T(8,128)S(1)} fusion(bf16[4,192,768]{2,1,0:T(8,128)(2,1)} %get-tuple-element.34, bf16[1024,768]{1,0:T(8,128)(2,1)S(1)} %copy-done), kind=kOutput, calls=%fused_computation.14 | convolution fusion | flops 1207959552 | bytes 5898240 | tf_op jit(solution)/shard_map/bte,de->btd/dot_general | solution.py:23
  85.7 1.5 fusion.6
  87.3 1.4 fusion.15
  89.3 6.6 %exchange_stream_2.1 = f32[1,24,1024]{2,1,0:T(8,128)} custom-call(bf16[4,1,24,1024]{3,2,1,0:T(8,128)(2,1)} %dynamic-slice_bitcast_fusion.refs_0_), custom_call_target="tpu_custom_call" | custom-call | tf_op jit(solution)/shard_map/exchange_stream_2/pallas_call | solution.py:102
  96.0 1.1 fusion.19
  97.9 1.0 convolution_convert_fusion.2
  99.0 2.0 %convolution_bitcast_fusion.1 = f32[128,768]{1,0:T(8,128)} fusion(bf16[4,192,768]{2,1,0:T(8,128)(2,1)S(1)} %copy-done.7, bf16[4,192,1024]{2,1,0:T(8,128)(2,1)} %copy-done.3, s32[]{:T(128)S(6)} %select_n.12), kind=kOutput, calls=%fused_computation.21 | convolution fusion | flops 150994944 | bytes 1769476 | tf_op jit(solution)/shard_map/btd,bte->de/dot_general | solution.py:23
  101.6 18.7 %conv_backward.1 = (bf16[6144,256]{1,0:T(8,128)(2,1)}, bf16[512,256]{1,0:T(8,128)(2,1)}, bf16[512,512]{1,0:T(8,128)(2,1)}, f32[1,24,1024]{2,1,0:T(8,128)}, f32[64,1024]{1,0:T(8,128)}) custom-call(s32[2]{0:T(128)} %pad_add_fusion.info_ref, bf16[512,256]{1,0:T(8,128)(2,1)} %copy-done.8, bf16[6144,256]{1,0:T(8,128)(2,1)} %bitcast.104, ...), custom_call_target="tpu_custom_call" | custom-call | tf_op jit(solution)/shard_map/conv_backward/pallas_call | solution.py:445
  120.4 1.7 %add_convert_fusion.1 = bf16[1,24,1024]{2,1,0:T(8,128)(2,1)} fusion(f32[1,24,1024]{2,1,0:T(8,128)} %get-tuple-element.36, bf16[24,256]{1,0:T(8,128)(2,1)S(1)} %copy-done.15, bf16[256,1024]{1,0:T(8,128)(2,1)S(1)} %copy-done.2), kind=kOutput, calls=%fused_computation.48 | convolution fusion | flops 12681216 | bytes 684032 | tf_op jit(solution)/shard_map/btc,cd->btd/dot_general | solution.py:23
  122.1 1.3 collective-permute-start.1
  123.4 1.3 dynamic-slice_convert_fusion.refs_2_
  124.7 3.6 %slice.18 = bf16[5632,256]{1,0:T(8,128)(2,1)} slice(bf16[6144,256]{1,0:T(8,128)(2,1)} %get-tuple-element.37), slice={[0:5632], [0:256]} | slice | bytes 5767168 | tf_op jit(solution)/shard_map/slice | solution.py:561
  128.3 11.6 %exchange_stream_3.1 = (bf16[128,512]{1,0:T(8,128)(2,1)}, bf16[64,256]{1,0:T(8,128)(2,1)}) custom-call(bf16[4,128,512]{2,1,0:T(8,128)(2,1)} %bitcast.112, bf16[4,64,256]{2,1,0:T(8,128)(2,1)} %bitcast.113), custom_call_target="tpu_custom_call" | custom-call | tf_op jit(solution)/shard_map/exchange_stream_3/pallas_call | solution.py:102
  139.9 20.0 %final_sums.1 = (f32[8,16,512]{2,1,0:T(8,128)}, f32[8,8,256]{2,1,0:T(8,128)}, f32[8,64,128]{2,1,0:T(8,128)}) custom-call(bf16[8,16,512]{2,1,0:T(8,128)(2,1)} %bitcast.117, bf16[8,8,256]{2,1,0:T(8,128)(2,1)} %bitcast.120, bf16[64,128]{1,0:T(8,128)(2,1)} %dynamic-slice_convert_fusion.refs_2_), custom_call_target="tpu_custom_call" | custom-call | tf_op jit(solution)/shard_map/final_sums/pallas_call | solution.py:389
  159.9 1.7 %bitcast_add_fusion = f32[64,1024]{1,0:T(8,128)} fusion(f32[64,1024]{1,0:T(8,128)S(1)} %copy-done.12, f32[8,64,128]{2,1,0:T(8,128)} %get-tuple-element.46), kind=kLoop, calls=%fused_computation.40 | loop fusion | flops 65536 | bytes 786432 | tf_op jit(solution)/shard_map/add | solution.py:579
  161.6 1.0 add_convert_fusion
  162.6 3.7 %maximum_bitcast_fusion = bf16[1,6144,256]{2,1,0:T(8,128)(2,1)} fusion(bf16[512,256]{1,0:T(8,128)(2,1)S(1)} %add_convert_fusion, bf16[5632,256]{1,0:T(8,128)(2,1)} %slice.18), kind=kLoop, calls=%fused_computation.11 | loop fusion | flops 6291456 | bytes 6291456 | tf_op jit(solution)/shard_map/broadcast_in_dim | solution.py:561
  (52 shorter events, 8.7 us)
Async XLA Ops:
  0.6 63.6 %copy-start = (bf16[1024,768]{1,0:T(8,128)(2,1)S(1)}, bf16[1024,768]{1,0:T(8,128)(2,1)}, u32[]{:S(2)}) copy-start(bf16[1024,768]{1,0:T(8,128)(2,1)} %param.13) | copy-start | bytes 4718596
  1.7 18.8 %collective-permute-start = (bf16[512,256]{1,0:T(8,128)(2,1)S(1)}, bf16[512,256]{1,0:T(8,128)(2,1)S(1)}, u32[]{:S(2)}, u32[]{:S(2)}) collective-permute-start(bf16[512,256]{1,0:T(8,128)(2,1)S(1)} %slice_bitcast_fusion), channel_id=1, source_target_pairs={{0,4},{4,8},{8,12},{12,16},{16,20},{20,24},{24,28},{1,5},{5,9},{9,... | collective-permute-start | bytes 786440 | tf_op jit(solution)/shard_map/ppermute | solution.py:476
  20.5 0.7 copy-start.8
  21.2 21.5 %copy-start.10 = (bf16[256,256]{1,0:T(8,128)(2,1)S(1)}, bf16[256,256]{1,0:T(8,128)(2,1)}, u32[]{:S(2)}) copy-start(bf16[256,256]{1,0:T(8,128)(2,1)} %param.11) | copy-start | bytes 393220
  21.2 41.0 %copy-start.2 = (bf16[256,1024]{1,0:T(8,128)(2,1)S(1)}, bf16[256,1024]{1,0:T(8,128)(2,1)}, u32[]{:S(2)}) copy-start(bf16[256,1024]{1,0:T(8,128)(2,1)} %param.12) | copy-start | bytes 1572868
  63.9 2.8 %copy-start.4 = (bf16[4,192,1024]{2,1,0:T(8,128)(2,1)}, bf16[4,192,1024]{2,1,0:T(8,128)(2,1)S(1)}, u32[]{:S(2)}) copy-start(bf16[4,192,1024]{2,1,0:T(8,128)(2,1)S(1)} %get-tuple-element.50) | copy-start | bytes 4718596
  64.2 2.5 %copy-start.3 = (bf16[4,192,1024]{2,1,0:T(8,128)(2,1)}, bf16[4,192,1024]{2,1,0:T(8,128)(2,1)S(1)}, u32[]{:S(2)}) copy-start(bf16[4,192,1024]{2,1,0:T(8,128)(2,1)S(1)} %fusion.2) | copy-start | bytes 4718596
  64.3 14.9 %copy-start.9 = (bf16[4,8,24,128]{3,2,1,0:T(8,128)(2,1)S(1)}, bf16[4,8,24,128]{3,2,1,0:T(8,128)(2,1)}, u32[]{:S(2)}) copy-start(bf16[4,8,24,128]{3,2,1,0:T(8,128)(2,1)} %get-tuple-element.42) | copy-start | bytes 589828
  64.3 16.9 %copy-start.1 = (bf16[256,1024]{1,0:T(8,128)(2,1)S(1)}, bf16[256,1024]{1,0:T(8,128)(2,1)}, u32[]{:S(2)}) copy-start(bf16[256,1024]{1,0:T(8,128)(2,1)} %param.14) | copy-start | bytes 1572868
  82.9 2.8 %copy-start.5 = (bf16[4,192,1024]{2,1,0:T(8,128)(2,1)S(1)}, bf16[4,192,1024]{2,1,0:T(8,128)(2,1)}, u32[]{:S(2)}) copy-start(bf16[4,192,1024]{2,1,0:T(8,128)(2,1)} %copy-done.4) | copy-start | bytes 4718596
  85.7 1.5 copy-start.6
  87.2 8.8 %copy-start.14 = (bf16[1,24,1024]{2,1,0:T(8,128)(2,1)S(1)}, bf16[1,24,1024]{2,1,0:T(8,128)(2,1)}, u32[]{:S(2)}) copy-start(bf16[1,24,1024]{2,1,0:T(8,128)(2,1)} %refs_0_.1) | copy-start | bytes 147460
  87.2 10.6 %copy-start.11 = (bf16[256,256]{1,0:T(8,128)(2,1)S(1)}, bf16[256,256]{1,0:T(8,128)(2,1)}, u32[]{:S(2)}) copy-start(bf16[256,256]{1,0:T(8,128)(2,1)} %param.11) | copy-start | bytes 393220
  87.2 11.7 %copy-start.7 = (bf16[4,192,768]{2,1,0:T(8,128)(2,1)S(1)}, bf16[4,192,768]{2,1,0:T(8,128)(2,1)}, u32[]{:S(2)}) copy-start(bf16[4,192,768]{2,1,0:T(8,128)(2,1)} %get-tuple-element.34) | copy-start | bytes 3538948
  101.6 18.7 %copy-start.15 = (bf16[24,256]{1,0:T(8,128)(2,1)S(1)}, bf16[24,256]{1,0:T(8,128)(2,1)}, u32[]{:S(2)}) copy-start(bf16[24,256]{1,0:T(8,128)(2,1)} %multiply_convert_fusion) | copy-start | bytes 36868
  122.1 39.5 %collective-permute-start.1 = (bf16[512,256]{1,0:T(8,128)(2,1)}, bf16[512,256]{1,0:T(8,128)(2,1)S(1)}, u32[]{:S(2)}, u32[]{:S(2)}) collective-permute-start(bf16[512,256]{1,0:T(8,128)(2,1)} %get-tuple-element.38), channel_id=1, source_target_pairs={{4,0},{8,4},{12,8},{16,12},{20,16},{24,20},{28,24},{5,1},{9,5},{13... | collective-permute-start | bytes 786440 | tf_op jit(solution)/shard_map/ppermute | solution.py:476
  124.7 35.2 %copy-start.12 = (f32[64,1024]{1,0:T(8,128)S(1)}, f32[64,1024]{1,0:T(8,128)}, u32[]{:S(2)}) copy-start(f32[64,1024]{1,0:T(8,128)} %get-tuple-element.45) | copy-start | bytes 786436
  162.6 3.7 %copy-start.13 = (f32[8,16,512]{2,1,0:T(8,128)S(1)}, f32[8,16,512]{2,1,0:T(8,128)}, u32[]{:S(2)}) copy-start(f32[8,16,512]{2,1,0:T(8,128)} %get-tuple-element.43) | copy-start | bytes 786436
  162.6 4.4 %copy-start.16 = (f32[8,8,256]{2,1,0:T(8,128)S(1)}, f32[8,8,256]{2,1,0:T(8,128)}, u32[]{:S(2)}) copy-start(f32[8,8,256]{2,1,0:T(8,128)} %get-tuple-element.44) | copy-start | bytes 196612
